TPU v7x, 512 devices: a whole 4x4x16 slice. The times are simulated.
512 devices in a mesh: dp: 128 (over y_lo, z, x), fsdp: 4 (over y_hi, core).
Axes of the slice: x: 4, y: 4 (y_hi: 2, y_lo: 2; y = y_hi * 2 + y_lo), z: 16, core: 2. Of those that a mesh axis runs over, the one named last changes fastest.
Arguments:
- cached: bfloat16 [128, 4, 256, 1024], P('dp', 'fsdp'), may hold values from -60 to 60
- send_rows: int32 [128, 4, 128, 4], P('dp', 'fsdp'), may hold values from -1 to 255, as said below
- take_rows: int32 [128, 4, 256], P('dp', 'fsdp'), may hold values from -1 to 511, as said below
- utt_index: int32 [128, 4, 256], P('dp', 'fsdp'), may hold values from 0 to 9, never falling along the last dimension, each value on 1 to 64 neighbouring positions
- upstream: bfloat16 [128, 4, 512, 1536], P('dp', 'fsdp'), may hold values from -6 to 6
- in_proj: bfloat16 [512, 1536], P(None, 'fsdp'), may hold values from -2 to 2
- norm_gain: bfloat16 [1536], P('fsdp'), may hold values from 0.099609375 to 1.8984375
- conv_kernel: bfloat16 [31, 1536], P(None, 'fsdp'), may hold values from -1 to 1
Outputs:
- grad_proj: float32 [512, 1536], P(None, 'fsdp')
- grad_kernel: float32 [31, 1536], P(None, 'fsdp')
- grad_gain: float32 [1536], P('fsdp')
- step_loss: float32 [128, 4], P('dp', 'fsdp')
Inputs may be any that keep to these rules, and one draw needn't show every extreme that they name: `send_rows`: entry [s, g, d, j] is -1 or the cache row of sender s (same fsdp group g) sent as entry j of its slot for device d. The used entries of a slot come first; a sender's used entries for one device lie in one aligned block of 4 cache rows; a sender's entries name distinct rows. Each device receives from 64 senders of its group, and some device of each group receives 4 rows from each of them. `take_rows`: entry [d, g, r] is -1 or s * 4 + j for a used entry send_rows[s, g, d, j]; each used entry is named once. The -1 entries of a device come last, the rows from one sender stand together, and some device of each group has no -1 entry. Sender 128 - 1 fills its whole slot for every device that it serves.
All inputs are finite; a program needn't handle non-finite values.
Results may differ from a plain program's by a relative error of at most 0.003.
Values may be sent and summed in bfloat16 or wider, within the bound.
A program may use at most 64 MiB of HBM per device.

v0:
```python
import jax
import jax.numpy as jnp
from jax import lax
from jax.sharding import PartitionSpec as P


def spread_conv(source_field, kernel_taps, tap_weights):
    tap_count = kernel_taps.shape[0]
    half_width = tap_count // 2
    step_count = source_field.shape[0]
    padded = jnp.pad(source_field, ((half_width, half_width), (0, 0)))
    summed = jnp.zeros_like(source_field)
    for offset in range(tap_count):
        summed = summed + kernel_taps[offset] * (
            tap_weights[:, offset : offset + 1] * padded[offset : offset + step_count]
        )
    return summed


def build_mask(live_steps, utterances, tap_count):
    half_width = tap_count // 2
    step_count = live_steps.shape[0]
    live_pad = jnp.pad(live_steps, (half_width, half_width))
    utter_pad = jnp.pad(utterances, (half_width, half_width), constant_values=-1)
    columns = []
    for offset in range(tap_count):
        columns.append(
            live_steps
            & live_pad[offset : offset + step_count]
            & (utterances == utter_pad[offset : offset + step_count])
        )
    return jnp.stack(columns, axis=1).astype(jnp.float32)


def layer_terms(encoded, live_steps, utterances, grad_above, gain, kernel):
    tap_count = kernel.shape[0]
    half_width = tap_count // 2
    step_count = encoded.shape[0]
    tap_weights = build_mask(live_steps, utterances, tap_count)
    row_mean = jnp.mean(encoded, axis=1, keepdims=True)
    centered = encoded - row_mean
    row_var = jnp.mean(centered * centered, axis=1, keepdims=True)
    inv_std = lax.rsqrt(row_var + 1e-05)
    normalized = centered * inv_std
    gain_f32 = gain.astype(jnp.float32)
    kernel_taps = kernel.astype(jnp.float32)
    normed = normalized * gain_f32
    conv_out = spread_conv(normed, kernel_taps, tap_weights)
    gate_sig = jax.nn.sigmoid(conv_out)
    output = encoded + conv_out * gate_sig
    scale = (encoded.shape[0] * encoded.shape[1]) ** (-0.5)
    grad_out = (
        jnp.where(live_steps[:, None], grad_above.astype(jnp.float32), jnp.zeros((), jnp.float32))
        * scale
    )
    device_loss = jnp.sum(output * grad_out)
    grad_conv = grad_out * (gate_sig * (1.0 + conv_out * (1.0 - gate_sig)))
    grad_normed = spread_conv(grad_conv, kernel_taps[::-1], tap_weights)
    padded = jnp.pad(normed, ((half_width, half_width), (0, 0)))
    grad_taps = jnp.stack(
        [
            jnp.sum(
                grad_conv
                * tap_weights[:, offset : offset + 1]
                * padded[offset : offset + step_count],
                axis=0,
            )
            for offset in range(tap_count)
        ]
    )
    grad_scale = jnp.sum(grad_normed * normalized, axis=0)
    grad_hat = grad_normed * gain_f32
    grad_x = grad_out + inv_std * (
        grad_hat
        - jnp.mean(grad_hat, axis=1, keepdims=True)
        - normalized * jnp.mean(grad_hat * normalized, axis=1, keepdims=True)
    )
    return (device_loss, grad_x.astype(jnp.bfloat16), grad_taps, grad_scale)


def per_device(cached, send_rows, take_rows, utt_index, upstream, in_proj, norm_gain, conv_kernel):
    cache_rows = cached[0, 0]
    wanted = send_rows[0, 0]
    outgoing = jnp.where(
        (wanted >= 0)[:, :, None],
        cache_rows[jnp.maximum(wanted, 0)],
        jnp.zeros((), cache_rows.dtype),
    )
    proj_full, taps_full, gain_full = (
        lax.all_gather(in_proj, "fsdp", axis=1, tiled=True),
        lax.all_gather(conv_kernel, "fsdp", axis=1, tiled=True),
        lax.all_gather(norm_gain[None, :], "fsdp", axis=1, tiled=True),
    )
    take_list = take_rows[0, 0]
    is_live = take_list >= 0
    safe_index = jnp.maximum(take_list, 0)
    pair_count = take_list.shape[0]
    step_width = cache_rows.shape[1] // 2
    arrived = lax.all_to_all(outgoing, "dp", split_axis=0, concat_axis=0, tiled=True)
    flat_rows = arrived.reshape(-1, arrived.shape[2])
    work_rows = jnp.where(is_live[:, None], flat_rows[safe_index], jnp.zeros((), flat_rows.dtype))
    frames = work_rows.reshape(2 * pair_count, step_width)
    encoded = jnp.dot(frames, proj_full, preferred_element_type=jnp.float32)
    live_steps = jnp.repeat(is_live, 2)
    utterances = jnp.repeat(utt_index[0, 0], 2)
    device_loss, grad_x, grad_taps, grad_scale = layer_terms(
        encoded, live_steps, utterances, upstream[0, 0], gain_full[0], taps_full
    )
    grad_weight = lax.dot_general(
        frames, grad_x, (((0,), (0,)), ((), ())), preferred_element_type=jnp.float32
    )
    shard_cols = in_proj.shape[1]
    totals = lax.psum((grad_weight, grad_taps, grad_scale[None, :]), ("dp", "fsdp"))
    col_start = lax.axis_index("fsdp") * shard_cols
    weight_part, taps_part, scale_part = [
        lax.dynamic_slice_in_dim(summed_item, col_start, shard_cols, 1) for summed_item in totals
    ]
    return (weight_part, taps_part, scale_part[0], device_loss.reshape(1, 1))


def solution(mesh):
    placed = (
        P("dp", "fsdp", None, None),
        P("dp", "fsdp", None, None),
        P("dp", "fsdp", None),
        P("dp", "fsdp", None),
        P("dp", "fsdp", None, None),
        P(None, "fsdp"),
        P("fsdp"),
        P(None, "fsdp"),
    )
    return jax.shard_map(
        per_device,
        mesh=mesh,
        in_specs=placed,
        out_specs=(P(None, "fsdp"), P(None, "fsdp"), P("fsdp"), P("dp", "fsdp")),
        check_vma=False,
    )
```

profile of v0, /device:TPU:8, one launch (start us, length us, event | category | flops | bytes accessed | tf_op | source)
XLA Modules:
  0.0 668.7 jit_solution(1528004560381405543)
XLA Ops:
  7.2 0.0 copy-start
  7.2 0.7 broadcast_maximum_fusion
  7.9 0.7 compare_bitcast_fusion
  8.6 0.1 copy.16
  8.7 0.1 reshape.100
  8.8 0.0 copy-done
  8.9 2.1 gather_fusion
  10.9 0.0 copy-start.5
  10.9 0.0 copy-start.3
  10.9 0.4 reshape.99
  11.4 0.0 copy-start.4
  11.4 0.0 copy-start.2
  11.4 0.1 copy.15
  11.5 1.5 broadcast_select_fusion
  13.1 20.7 %all-to-all-start = ((bf16[128,4,1024]{2,1,0:T(4,128)(2,1)}), bf16[128,4,1024]{2,1,0:T(4,128)(2,1)S(1)}, u32[]{:S(2)}, u32[]{:S(2)}) async-start(bf16[128,4,1024]{2,1,0:T(4,128)(2,1)} %broadcast_select_fusion), calls=%async_computation | async-start | bytes 2097152 | tf_op jit(solution)/shard_map/all_to_all | solution.py:99
  33.7 0.0 all-gather.4.cloned.1.call-start
  33.8 0.7 all-gather.4.cloned.1.call-update
  34.5 0.0 all-reduce.7.cloned.1.call-start
  34.5 0.0 copy-done.5
  34.6 0.1 broadcast_in_dim.62
  34.7 0.2 broadcast_in_dim.63
  34.8 0.0 copy-done.3
  34.8 0.1 broadcast_in_dim.70
  34.9 0.1 reshape.94
  35.1 0.1 fusion.58
  35.3 0.1 fusion.50
  35.5 0.1 fusion.42
  35.7 0.1 fusion.66
  35.8 0.1 broadcast_in_dim.71
  36.0 0.2 and.227
  36.1 0.2 stack.220
  36.3 0.0 copy-done.4
  36.3 6.7 %all-gather.1 = bf16[4,1,384]{2,1,0:T(2,128)(2,1)S(1)} all-gather(bf16[1,1,384]{2,1,0:T(2,128)(2,1)S(1)} %reshape.120), channel_id=2, replica_groups=mesh['dp'=128,'fsdp'=4] {'fsdp'}, dimensions={0}, use_global_device_ids=true | all-gather | bytes 3840 | tf_op jit(solution)/shard_map/all_gather | solution.py:92
  43.1 0.0 copy-done.2
  43.1 7.0 %all_gather.10 = bf16[31,1536]{1,0:T(8,128)(2,1)S(1)} all-gather(bf16[31,384]{1,0:T(8,128)(2,1)S(1)} %copy-done.2), channel_id=1, replica_groups=mesh['dp'=128,'fsdp'=4] {'fsdp'}, dimensions={1}, use_global_device_ids=true | all-gather | bytes 119040 | tf_op jit(solution)/shard_map/all_gather | solution.py:91
  50.1 0.2 slice_reduce_fusion.29
  50.3 0.3 slice_reduce_fusion.30
  50.7 39.2 %all-to-all-done = bf16[128,4,1024]{2,1,0:T(4,128)(2,1)S(1)} async-done(((bf16[128,4,1024]{2,1,0:T(4,128)(2,1)}), bf16[128,4,1024]{2,1,0:T(4,128)(2,1)S(1)}, u32[]{:S(2)}, u32[]{:S(2)}) %all-to-all-start) | async-done | bytes 1048608 | tf_op jit(solution)/shard_map/all_to_all | solution.py:99
  89.9 0.3 reshape.93
  90.2 1.2 gather_fusion.1
  91.3 0.2 gather.10
  91.5 0.0 all-gather.4.cloned.1.call-done
  91.6 2.5 fusion.109
  94.1 0.5 multiply_reduce_fusion.33
  94.6 0.0 copy-start.1
  94.6 0.5 fusion.8
  95.0 0.9 copy-done.1
  96.0 31.9 %multiply_reduce_fusion.1 = (f32[1536]{0:T(1024)S(1)}, f32[1536]{0:T(1024)S(1)}, f32[1536]{0:T(1024)S(1)}, f32[1536]{0:T(1024)S(1)}, f32[1536]{0:T(1024)S(1)}, /...) fusion(f32[512,1536]{1,0:T(8,128)S(1)} %fusion.8, ...), kind=kLoop, calls=%fused_computation.10 | loop fusion | flops 102222336 | bytes 11319808 | tf_op jit(solution)/shard_map/reduce_sum | solution.py:62
  127.9 6.8 %multiply_reduce_fusion.10 = (f32[1536]{0:T(1024)S(1)}, f32[1536]{0:T(1024)S(1)}, f32[1536]{0:T(1024)S(1)}, f32[1536]{0:T(1024)S(1)}, f32[1536]{0:T(1024)S(1)}, ...) fusion(f32[512,1536]{1,0:T(8,128)S(1)} %get-tuple-element.72, ...), kind=kLoop, calls=%fused_computation.19 | loop fusion | flops 21219840 | bytes 6365184 | tf_op jit(solution)/shard_map/reduce_sum | solution.py:62
  134.7 6.6 multiply_reduce_fusion.16
  141.3 3.1 multiply_reduce_fusion.20
  144.8 28.3 %multiply_reduce_fusion = (f32[1536]{0:T(1024)S(1)}, f32[512]{0:T(512)S(1)}, f32[512]{0:T(512)S(1)}, f32[]{:T(128)}, f32[512,1536]{1,0:T(8,128)S(1)}) fusion(f32[512,1536]{1,0:T(8,128)S(1)} %get-tuple-element.137, f32[512]{0:T(512)S(1)} %add_rsqrt_fusion, f32[512]{0:T(512)S(1)} %broadcast_multiply_fusion.2, f32[1536]{0:T(1024)S(1)} %reshape.122, ...), kind=kLoop, calls=%fused_computation.9 | loop fusion | flops 86504960 | bytes 14430724 | tf_op jit(solution)/shard_map/reduce_sum | solution.py:71
  173.0 3.6 fusion.9
  176.6 2.8 stack.252
  179.4 0.0 all-reduce.7.cloned.1.call-update
  179.4 99.5 %psum.23 = f32[1,1536]{1,0:T(1,128)S(1)} all-reduce(f32[1,1536]{1,0:T(1,128)S(1)} %broadcast_in_dim.73), channel_id=1, replica_groups=mesh['dp'=128,'fsdp'=4] {'dp','fsdp'}, use_global_device_ids=true, to_apply=%region_38.39 | all-reduce | flops 1536 | bytes 12288 | tf_op jit(solution)/shard_map/psum | solution.py:113
  278.9 0.6 dynamic-slice_reduce_fusion
  279.5 378.9 %all-reduce.7.cloned.1.call-done = (f32[512,1536]{1,0:T(8,128)}, f32[31,1536]{1,0:T(8,128)}) async-done(((f32[512,1536]{1,0:T(8,128)}, f32[31,1536]{1,0:T(8,128)}), (f32[512,1536]{1,0:T(8,128)}, f32[31,1536]{1,0:T(8,128)})) %all-reduce.7.cloned.1.call-update) | async-done | bytes 3336208 | tf_op jit(solution)/shard_map/psum | solution.py:113
  658.4 2.1 constant_dynamic-slice_fusion.1
  660.4 1.4 constant_dynamic-slice_fusion
  (77 shorter events, 0.6 us)
Async XLA Ops:
  7.2 1.7 copy-start
  10.9 23.6 %copy-start.5 = (s32[1,1,256]{2,1,0:T(1,128)S(1)}, s32[1,1,256]{2,1,0:T(1,128)}, u32[]{:S(2)}) copy-start(s32[1,1,256]{2,1,0:T(1,128)} %param.10) | copy-start | bytes 3076
  10.9 23.9 %copy-start.3 = (s32[1,1,256]{2,1,0:T(1,128)S(1)}, s32[1,1,256]{2,1,0:T(1,128)}, u32[]{:S(2)}) copy-start(s32[1,1,256]{2,1,0:T(1,128)} %param.11) | copy-start | bytes 3076
  11.4 24.9 %copy-start.4 = (bf16[384]{0:T(512)(128)(2,1)S(1)}, bf16[384]{0:T(512)(128)(2,1)}, u32[]{:S(2)}) copy-start(bf16[384]{0:T(512)(128)(2,1)} %param.14) | copy-start | bytes 2308
  11.4 31.7 %copy-start.2 = (bf16[31,384]{1,0:T(8,128)(2,1)S(1)}, bf16[31,384]{1,0:T(8,128)(2,1)}, u32[]{:S(2)}) copy-start(bf16[31,384]{1,0:T(8,128)(2,1)} %param.15) | copy-start | bytes 71428
  13.1 76.8 %all-to-all-start = ((bf16[128,4,1024]{2,1,0:T(4,128)(2,1)}), bf16[128,4,1024]{2,1,0:T(4,128)(2,1)S(1)}, u32[]{:S(2)}, u32[]{:S(2)}) async-start(bf16[128,4,1024]{2,1,0:T(4,128)(2,1)} %broadcast_select_fusion), calls=%async_computation | async-start | bytes 2097152 | tf_op jit(solution)/shard_map/all_to_all | solution.py:99
  33.7 57.8 %all-gather.4.cloned.1.call-start = ((), (), s32[]{:S(2)}) async-start(), calls=%async_computation.1 | async-start | bytes 1966080 | tf_op jit(solution)/shard_map/all_gather | solution.py:90
  34.5 623.9 %all-reduce.7.cloned.1.call-start = ((), (), s32[]{:S(2)}) async-start(), calls=%async_computation.2 | async-start | bytes 6684672 | tf_op jit(solution)/shard_map/psum | solution.py:113
  94.6 1.4 copy-start.1
Sparse Core Ops, SparseCore 0:
  36.7 33.4 all-gather.3
  179.5 478.7 all-reduce.6
where the time goes:
time: 669 us
  waiting for transfers between devices  419 us (63%)
  blocking collectives  113 us (17%)
  other arithmetic  80.9 us (12%)
  starting transfers between devices  20.7 us (3%)
  between operations  14.8 us (2%)
  local copies, waits for them, and re-layouts  14.2 us (2%)
    psum x1, waiting for transfers between devices, per_device(): lax.psum((grad_weight, grad_taps, grad_scale[None, :]), ('dp', 'fsdp'))  379 us
    psum x1, blocking collectives, per_device(): lax.psum((grad_weight, grad_taps, grad_scale[None, :]), ('dp', 'fsdp'))  99.5 us
    reduce_sum x4, other arithmetic, layer_terms(): jnp.sum(grad_conv * tap_weights[:, offset:offset + 1] * padded[offset:off...  48.3 us
    all_to_all x1, waiting for transfers between devices, per_device(): lax.all_to_all(outgoing, 'dp', split_axis=0, concat_axis=0, tiled=True)  39.2 us
    reduce_sum x1, other arithmetic, layer_terms(): grad_scale = jnp.sum(grad_normed * normalized, axis=0)  28.3 us
    all_to_all x1, starting transfers between devices, per_device(): lax.all_to_all(outgoing, 'dp', split_axis=0, concat_axis=0, tiled=True)  20.7 us
  transfers between devices with their start and end apart: 3, of which 2 were waited for; matrix products, arithmetic and copies ran while one was open for 1% of the time, Pallas kernels for 0%

commit v1 on v0

--- a/solution.py
+++ b/solution.py
@@ -1,7 +1,21 @@
+import functools
+
 import jax
 import jax.numpy as jnp
 from jax import lax
+from jax.experimental import pallas as pl
+from jax.experimental.pallas import tpu as pltpu
 from jax.sharding import PartitionSpec as P
+
+LANES = 128
+RING = 4
+Z_SIZE = 16
+UNIT = 16
+Z_OWNERS = 13
+X_ROWS = Z_OWNERS * UNIT
+Y_ROWS = RING * X_ROWS
+Q_ROWS = 2 * Y_ROWS
+MESH_ID = pl.DeviceIdType.MESH
 
 
 def spread_conv(source_field, kernel_taps, tap_weights):
@@ -78,14 +92,246 @@
     return (device_loss, grad_x.astype(jnp.bfloat16), grad_taps, grad_scale)
 
 
+def reduce_kernel(
+    g_ref, o_ref,
+    cbuf, ysend, ystage, yfirst, yfrom,
+    xbuf, xstage, xfirst, xfrom,
+    zbuf, zfrom, final,
+    core_s, core_r, y_s, y_r, x_s, x_r, z_s, z_r, za_s, za_r, xa_s, xa_r, ya_s, ya_r,
+):
+    p = lax.axis_index("dp")
+    f = lax.axis_index("fsdp")
+    x = lax.rem(p, RING)
+    z = lax.rem(lax.div(p, RING), Z_SIZE)
+    y_lo = lax.div(p, RING * Z_SIZE)
+    y_hi = lax.div(f, 2)
+    core = lax.rem(f, 2)
+    y = y_hi * 2 + y_lo
+
+    def at(yy, zz, xx, cc):
+        return (
+            (lax.rem(yy, 2) * Z_SIZE + zz) * RING + xx,
+            lax.div(yy, 2) * 2 + cc,
+        )
+
+    y_r1, y_l1, y_op = lax.rem(y + 1, RING), lax.rem(y + 3, RING), lax.rem(y + 2, RING)
+    x_r1, x_l1, x_op = lax.rem(x + 1, RING), lax.rem(x + 3, RING), lax.rem(x + 2, RING)
+    y_mate = y_hi * 2 + 1 - y_lo
+    dev_core = at(y, z, x, 1 - core)
+    dev_yr, dev_yl = at(y_r1, z, x, core), at(y_l1, z, x, core)
+    dev_xr, dev_xl = at(y, z, x_r1, core), at(y, z, x_l1, core)
+    dev_mate = at(y_mate, z, x, core)
+
+    def dev_z(o):
+        return at(y, lax.rem(z + o, Z_SIZE), x, core)
+
+    barrier = pltpu.get_barrier_semaphore()
+    for d in [dev_core, dev_yr, dev_yl, dev_xr, dev_xl]:
+        pl.semaphore_signal(barrier, inc=1, device_id=d, device_id_type=MESH_ID)
+    for o in range(1, Z_SIZE):
+        pl.semaphore_signal(barrier, inc=1, device_id=dev_z(o), device_id_type=MESH_ID)
+    pl.semaphore_wait(barrier, 5 + Z_SIZE - 1)
+
+    def send(src, dst, ssem, rsem, d):
+        copy = pltpu.make_async_remote_copy(
+            src_ref=src, dst_ref=dst, send_sem=ssem, recv_sem=rsem,
+            device_id=d, device_id_type=MESH_ID,
+        )
+        copy.start()
+        return copy
+
+    def piece(yy, cc):
+        row = (lax.div(yy, 2) * 2 + cc) * Q_ROWS + lax.rem(yy, 2) * Y_ROWS
+        return pl.ds(pl.multiple_of(row, UNIT), Y_ROWS)
+
+    core_copies = []
+    for o in (2, 1, 3, 0):
+        yy = lax.rem(y + o, RING)
+        core_copies.append(
+            send(g_ref.at[piece(yy, 1 - core)], cbuf.at[o], core_s.at[o], core_r.at[o], dev_core)
+        )
+    half = Y_ROWS // 2
+    lo, hi = pl.ds(0, half), pl.ds(half, half)
+
+    def summed(o):
+        return g_ref[piece(lax.rem(y + o, RING), core)] + cbuf[o]
+
+    core_copies[0].wait_recv()
+    ysend[1] = summed(2).astype(jnp.bfloat16)
+    y0 = send(ysend.at[1, lo], yfirst.at[0], y_s.at[0], y_r.at[0], dev_yr)
+    y1 = send(ysend.at[1, hi], yfirst.at[1], y_s.at[1], y_r.at[1], dev_yl)
+    core_copies[1].wait_recv()
+    ysend[0] = summed(1).astype(jnp.bfloat16)
+    y2 = send(ysend.at[0, hi], yfrom.at[0, hi], y_s.at[2], y_r.at[2], dev_yr)
+    core_copies[2].wait_recv()
+    ysend[2] = summed(3).astype(jnp.bfloat16)
+    y3 = send(ysend.at[2, lo], yfrom.at[1, lo], y_s.at[3], y_r.at[3], dev_yl)
+    core_copies[3].wait_recv()
+    y0.wait_recv()
+    part = g_ref[piece(y_r1, core)] + cbuf[1]
+    ystage[0] = (part[:half] + yfirst[0].astype(jnp.float32)).astype(jnp.bfloat16)
+    y4 = send(ystage.at[0], yfrom.at[0, lo], y_s.at[4], y_r.at[4], dev_yr)
+    y1.wait_recv()
+    part = g_ref[piece(y_l1, core)] + cbuf[3]
+    ystage[1] = (part[half:] + yfirst[1].astype(jnp.float32)).astype(jnp.bfloat16)
+    y5 = send(ystage.at[1], yfrom.at[1, hi], y_s.at[5], y_r.at[5], dev_yl)
+    for copy in (y2, y3, y4, y5):
+        copy.wait_recv()
+    xbuf[...] = (
+        summed(0) + yfrom[0].astype(jnp.float32) + yfrom[1].astype(jnp.float32)
+    ).reshape(RING, X_ROWS, LANES)
+
+    xh = X_ROWS // 2
+    xlo, xhi = pl.ds(0, xh), pl.ds(xh, xh)
+    x0 = send(xbuf.at[x_op, xlo], xfirst.at[0], x_s.at[0], x_r.at[0], dev_xr)
+    x1 = send(xbuf.at[x_op, xhi], xfirst.at[1], x_s.at[1], x_r.at[1], dev_xl)
+    x2 = send(xbuf.at[x_r1, xhi], xfrom.at[0, xhi], x_s.at[2], x_r.at[2], dev_xr)
+    x3 = send(xbuf.at[x_l1, xlo], xfrom.at[1, xlo], x_s.at[3], x_r.at[3], dev_xl)
+    x0.wait_recv()
+    xstage[0] = xbuf[x_r1, xlo] + xfirst[0]
+    x4 = send(xstage.at[0], xfrom.at[0, xlo], x_s.at[4], x_r.at[4], dev_xr)
+    x1.wait_recv()
+    xstage[1] = xbuf[x_l1, xhi] + xfirst[1]
+    x5 = send(xstage.at[1], xfrom.at[1, xhi], x_s.at[5], x_r.at[5], dev_xl)
+    for copy in (x2, x3, x4, x5):
+        copy.wait_recv()
+    zbuf[...] = (xbuf[x] + xfrom[0] + xfrom[1]).reshape(Z_OWNERS, UNIT, LANES)
+
+    def z_copy(o):
+        to = lax.rem(z + o, Z_SIZE)
+        return pltpu.make_async_remote_copy(
+            src_ref=zbuf.at[lax.min(to, Z_OWNERS - 1)],
+            dst_ref=zfrom.at[o - 1],
+            send_sem=z_s.at[o - 1],
+            recv_sem=z_r.at[o - 1],
+            device_id=dev_z(o),
+            device_id_type=MESH_ID,
+        )
+
+    def own_rows(zz):
+        row = y_lo * Y_ROWS + x * X_ROWS + lax.min(zz, Z_OWNERS - 1) * UNIT
+        return final.at[pl.ds(pl.multiple_of(row, UNIT), UNIT)]
+
+    def za_copy(o, zz):
+        return pltpu.make_async_remote_copy(
+            src_ref=own_rows(zz),
+            dst_ref=own_rows(zz),
+            send_sem=za_s.at[o - 1],
+            recv_sem=za_r.at[o - 1],
+            device_id=dev_z(o),
+            device_id_type=MESH_ID,
+        )
+
+    for o in range(1, Z_SIZE):
+        @pl.when(lax.rem(z + o, Z_SIZE) < Z_OWNERS)
+        def _():
+            z_copy(o).start()
+
+    @pl.when(z < Z_OWNERS)
+    def _():
+        total = zbuf[lax.min(z, Z_OWNERS - 1)]
+        for o in range(1, Z_SIZE):
+            z_copy(o).wait_recv()
+            total = total + zfrom[o - 1]
+        row = y_lo * Y_ROWS + x * X_ROWS + lax.min(z, Z_OWNERS - 1) * UNIT
+        final[pl.ds(pl.multiple_of(row, UNIT), UNIT)] = total.astype(jnp.bfloat16)
+        for o in range(1, Z_SIZE):
+            za_copy(o, z).start()
+
+    for o in range(1, Z_SIZE):
+        source = lax.rem(z + Z_SIZE - o, Z_SIZE)
+        @pl.when(source < Z_OWNERS)
+        def _():
+            za_copy(o, source).wait_recv()
+
+    def rows(xx, start, size):
+        row = y_lo * Y_ROWS + xx * X_ROWS + start
+        return final.at[pl.ds(pl.multiple_of(row, UNIT), size)]
+
+    cut = 7 * UNIT
+    mine = rows(x, 0, X_ROWS)
+    a0 = send(mine, mine, xa_s.at[0], xa_r.at[0], dev_xr)
+    a1 = send(mine, mine, xa_s.at[1], xa_r.at[1], dev_xl)
+    b0 = send(mine, mine, ya_s.at[0], ya_r.at[0], dev_mate)
+    a0.wait_recv()
+    ring_lo = rows(x_l1, 0, cut)
+    a2 = send(ring_lo, ring_lo, xa_s.at[2], xa_r.at[2], dev_xr)
+    got = rows(x_l1, 0, X_ROWS)
+    b1 = send(got, got, ya_s.at[1], ya_r.at[1], dev_mate)
+    a1.wait_recv()
+    ring_hi = rows(x_r1, cut, X_ROWS - cut)
+    a3 = send(ring_hi, ring_hi, xa_s.at[3], xa_r.at[3], dev_xl)
+    got = rows(x_r1, 0, X_ROWS)
+    b2 = send(got, got, ya_s.at[2], ya_r.at[2], dev_mate)
+    a2.wait_recv()
+    a3.wait_recv()
+    got = rows(x_op, 0, X_ROWS)
+    b3 = send(got, got, ya_s.at[3], ya_r.at[3], dev_mate)
+    for copy in (b0, b1, b2, b3):
+        copy.wait_recv()
+
+    tile_rows = o_ref.shape[0]
+    for i in range(o_ref.shape[1] // LANES):
+        o_ref[:, i * LANES : (i + 1) * LANES] = final[
+            i * tile_rows : (i + 1) * tile_rows
+        ].astype(jnp.float32)
+
+    for copy in core_copies + [y0, y1, y2, y3, y4, y5, x0, x1, x2, x3, x4, x5]:
+        copy.wait_send()
+    for o in range(1, Z_SIZE):
+        @pl.when(lax.rem(z + o, Z_SIZE) < Z_OWNERS)
+        def _():
+            z_copy(o).wait_send()
+
+    @pl.when(z < Z_OWNERS)
+    def _():
+        for o in range(1, Z_SIZE):
+            za_copy(o, z).wait_send()
+    for copy in (a0, a1, a2, a3, b0, b1, b2, b3):
+        copy.wait_send()
+
+
+def reduce_gradients(packed, rows, cols):
+    f32, bf16 = jnp.float32, jnp.bfloat16
+    half, xh = Y_ROWS // 2, X_ROWS // 2
+    dma = pltpu.SemaphoreType.DMA
+    return pl.pallas_call(
+        reduce_kernel,
+        out_shape=jax.ShapeDtypeStruct((rows, cols), f32),
+        in_specs=[pl.BlockSpec(memory_space=pltpu.VMEM)],
+        out_specs=pl.BlockSpec(memory_space=pltpu.VMEM),
+        scratch_shapes=[
+            pltpu.VMEM((RING, Y_ROWS, LANES), f32),
+            pltpu.VMEM((3, Y_ROWS, LANES), bf16),
+            pltpu.VMEM((2, half, LANES), bf16),
+            pltpu.VMEM((2, half, LANES), bf16),
+            pltpu.VMEM((2, Y_ROWS, LANES), bf16),
+            pltpu.VMEM((RING, X_ROWS, LANES), f32),
+            pltpu.VMEM((2, xh, LANES), f32),
+            pltpu.VMEM((2, xh, LANES), f32),
+            pltpu.VMEM((2, X_ROWS, LANES), f32),
+            pltpu.VMEM((Z_OWNERS, UNIT, LANES), f32),
+            pltpu.VMEM((Z_SIZE - 1, UNIT, LANES), f32),
+            pltpu.VMEM((Q_ROWS, LANES), bf16),
+            dma((RING,)), dma((RING,)),
+            dma((6,)), dma((6,)),
+            dma((6,)), dma((6,)),
+            dma((Z_SIZE - 1,)), dma((Z_SIZE - 1,)),
+            dma((Z_SIZE - 1,)), dma((Z_SIZE - 1,)),
+            dma((4,)), dma((4,)),
+            dma((4,)), dma((4,)),
+        ],
+        compiler_params=pltpu.CompilerParams(
+            collective_id=0, has_side_effects=True, vmem_limit_bytes=40 << 20
+        ),
+        name="reduce_gradients",
+    )(packed)
+
+
 def per_device(cached, send_rows, take_rows, utt_index, upstream, in_proj, norm_gain, conv_kernel):
     cache_rows = cached[0, 0]
     wanted = send_rows[0, 0]
-    outgoing = jnp.where(
-        (wanted >= 0)[:, :, None],
-        cache_rows[jnp.maximum(wanted, 0)],
-        jnp.zeros((), cache_rows.dtype),
-    )
+    outgoing = cache_rows[jnp.maximum(wanted, 0)]
     proj_full, taps_full, gain_full = (
         lax.all_gather(in_proj, "fsdp", axis=1, tiled=True),
         lax.all_gather(conv_kernel, "fsdp", axis=1, tiled=True),
@@ -109,13 +355,21 @@
     grad_weight = lax.dot_general(
         frames, grad_x, (((0,), (0,)), ((), ())), preferred_element_type=jnp.float32
     )
-    shard_cols = in_proj.shape[1]
-    totals = lax.psum((grad_weight, grad_taps, grad_scale[None, :]), ("dp", "fsdp"))
-    col_start = lax.axis_index("fsdp") * shard_cols
-    weight_part, taps_part, scale_part = [
-        lax.dynamic_slice_in_dim(summed_item, col_start, shard_cols, 1) for summed_item in totals
-    ]
-    return (weight_part, taps_part, scale_part[0], device_loss.reshape(1, 1))
+    depth, width = grad_weight.shape
+    taps = grad_taps.shape[0]
+    rows = depth + taps + 1
+    quarters = width // in_proj.shape[1]
+    stacked = jnp.concatenate([grad_weight, grad_taps, grad_scale[None, :]], axis=0)
+    tiles = stacked.reshape(rows, width // LANES, LANES).transpose(1, 0, 2)
+    packed = tiles.reshape(quarters, -1, LANES)
+    packed = jnp.pad(packed, ((0, 0), (0, Q_ROWS - packed.shape[1]), (0, 0)))
+    total = reduce_gradients(packed.reshape(-1, LANES), rows, in_proj.shape[1])
+    return (
+        total[:depth],
+        total[depth : depth + taps],
+        total[depth + taps],
+        device_loss.reshape(1, 1),
+    )
 
 
 def solution(mesh):

time: 669 us -> 315 us (0.47)
  waiting for transfers between devices: 419 us -> 39.7 us
  blocking collectives: 113 us -> 13.7 us
  Pallas kernels: 0 us -> 49.9 us
  local copies, waits for them, and re-layouts: 14.2 us -> 54.4 us
  other arithmetic: 80.9 us -> 115 us
    psum x1 -> x0, waiting for transfers between devices: 379 us -> none  [per_device(): lax.psum((grad_weight, grad_taps, grad_scale[None, :]), ('dp', 'fsdp'))]
    psum x1 -> x0, blocking collectives: 99.5 us -> none  [per_device(): lax.psum((grad_weight, grad_taps, grad_scale[None, :]), ('dp', 'fsdp'))]
    pallas_call x0 -> x1, Pallas kernels: none -> 49.9 us  [reduce_gradients(): pl.pallas_call(reduce_kernel, out_shape=jax.ShapeDtypeStruct((rows, cols)...]
    concatenate x0 -> x33, local copies, waits for them, and re-layouts: none -> 39.3 us  [per_device(): jnp.concatenate([grad_weight, grad_taps, grad_scale[None, :]], axis=0)]
    reduce_sum x1, other arithmetic: 28.3 us -> 59.1 us  [layer_terms(): grad_scale = jnp.sum(grad_normed * normalized, axis=0)]
  transfers between devices with their start and end apart: 3 -> 2, of which waited for: 2 -> 1; matrix products, arithmetic and copies ran while one was open for 1% -> 1% of each run, Pallas kernels for 0% -> 0%
where the time goes in v1:
time: 315 us; the launch traced here: 314 us
  other arithmetic  115 us (37%)
  local copies, waits for them, and re-layouts  54.4 us (17%)
  Pallas kernels  49.9 us (16%)
  waiting for transfers between devices  39.7 us (13%)
  starting transfers between devices  20.7 us (7%)
  between operations  15 us (5%)
  blocking collectives  13.7 us (4%)
  matrix products  5.25 us (2%)
    reduce_sum x1, other arithmetic, layer_terms(): grad_scale = jnp.sum(grad_normed * normalized, axis=0)  59.1 us
    reduce_sum x4, other arithmetic, layer_terms(): jnp.sum(grad_conv * tap_weights[:, offset:offset + 1] * padded[offset:off...  51.4 us
    pallas_call x1, Pallas kernels, reduce_gradients(): pl.pallas_call(reduce_kernel, out_shape=jax.ShapeDtypeStruct((rows, cols)...  49.9 us
    concatenate x33, local copies, waits for them, and re-layouts, per_device(): jnp.concatenate([grad_weight, grad_taps, grad_scale[None, :]], axis=0)  39.3 us
    all_to_all x1, waiting for transfers between devices, per_device(): lax.all_to_all(outgoing, 'dp', split_axis=0, concat_axis=0, tiled=True)  39 us
    all_to_all x1, starting transfers between devices, per_device(): lax.all_to_all(outgoing, 'dp', split_axis=0, concat_axis=0, tiled=True)  20.7 us
    all_gather x1, blocking collectives, per_device(): lax.all_gather(conv_kernel, 'fsdp', axis=1, tiled=True)  6.99 us
    all_gather x1, blocking collectives, per_device(): lax.all_gather(norm_gain[None, :], 'fsdp', axis=1, tiled=True)  6.66 us
  transfers between devices with their start and end apart: 2, of which 1 were waited for; matrix products, arithmetic and copies ran while one was open for 1% of the time, Pallas kernels for 0%

profile of v1, /device:TPU:8, one launch (start us, length us, event | category | flops | bytes accessed | tf_op | source)
XLA Modules:
  0.0 313.8 jit_solution(15434844009052463626)
XLA Ops:
  7.2 0.7 broadcast_maximum_fusion
  7.9 0.1 copy.17
  8.0 0.1 reshape.184
  8.2 2.0 gather_fusion
  10.3 1.2 reshape.183
  11.6 20.7 %all-to-all-start = ((bf16[128,4,1024]{2,1,0:T(4,128)(2,1)}), bf16[128,4,1024]{2,1,0:T(4,128)(2,1)S(1)}, u32[]{:S(2)}, u32[]{:S(2)}) async-start(bf16[128,4,1024]{2,1,0:T(4,128)(2,1)} %reshape.183), calls=%async_computation | async-start | bytes 2097152 | tf_op jit(solution)/shard_map/all_to_all | solution.py:345
  32.3 0.7 all-gather.4.cloned.1.call-update
  33.0 0.1 broadcast_in_dim.53
  33.1 0.2 broadcast_in_dim.54
  33.3 0.2 copy-done.41
  33.6 0.1 reshape.176
  34.6 0.2 and.226
  34.8 0.2 stack.155
  35.0 6.7 %all-gather.1 = bf16[4,1,384]{2,1,0:T(2,128)(2,1)S(1)} all-gather(bf16[1,1,384]{2,1,0:T(2,128)(2,1)S(1)} %reshape.204), channel_id=2, replica_groups=mesh['dp'=128,'fsdp'=4] {'fsdp'}, dimensions={0}, use_global_device_ids=true | all-gather | bytes 3840 | tf_op jit(solution)/shard_map/all_gather | solution.py:338
  41.7 7.0 %all_gather.10 = bf16[31,1536]{1,0:T(8,128)(2,1)S(1)} all-gather(bf16[31,384]{1,0:T(8,128)(2,1)S(1)} %copy-done.32), channel_id=1, replica_groups=mesh['dp'=128,'fsdp'=4] {'fsdp'}, dimensions={1}, use_global_device_ids=true | all-gather | bytes 119040 | tf_op jit(solution)/shard_map/all_gather | solution.py:337
  48.7 0.2 slice_reduce_fusion.29
  48.9 0.3 slice_reduce_fusion.30
  49.4 39.0 %all-to-all-done = bf16[128,4,1024]{2,1,0:T(4,128)(2,1)S(1)} async-done(((bf16[128,4,1024]{2,1,0:T(4,128)(2,1)}), bf16[128,4,1024]{2,1,0:T(4,128)(2,1)S(1)}, u32[]{:S(2)}, u32[]{:S(2)}) %all-to-all-start) | async-done | bytes 1048608 | tf_op jit(solution)/shard_map/all_to_all | solution.py:345
  88.4 0.3 reshape.175
  88.7 1.2 gather_fusion.1
  89.8 0.2 gather.10
  90.0 2.5 fusion.110
  92.6 0.4 multiply_reduce_fusion.33
  93.1 0.5 fusion.8
  93.5 0.7 copy-done.1
  94.3 0.8 copy-done.4
  95.1 32.9 %multiply_reduce_fusion.1 = (f32[1536]{0:T(1024)S(1)}, f32[1536]{0:T(1024)S(1)}, f32[1536]{0:T(1024)S(1)}, f32[1536]{0:T(1024)S(1)}, f32[1536]{0:T(1024)S(1)}, /...) fusion(f32[512,1536]{1,0:T(8,128)S(1)} %fusion.8, ...), kind=kLoop, calls=%fused_computation.10 | loop fusion | flops 102222336 | bytes 11319808 | tf_op jit(solution)/shard_map/reduce_sum | solution.py:76
  128.0 7.3 %multiply_reduce_fusion.10 = (f32[1536]{0:T(1024)}, f32[1536]{0:T(1024)}, f32[1536]{0:T(1024)}, f32[1536]{0:T(1024)}, f32[1536]{0:T(1024)}, /*index=5*/f32[1536]...) fusion(f32[512,1536]{1,0:T(8,128)S(1)} %get-tuple-element.70, f32[512,1536]{1,0:T(8,128)S(1)} %fusion.8, ...), kind=kLoop, calls=%fused_computation.19 | loop fusion | flops 21219840 | bytes 6365184 | tf_op jit(solution)/shard_map/reduce_sum | solution.py:76
  135.3 7.3 %multiply_reduce_fusion.16 = (f32[1536]{0:T(1024)}, f32[1536]{0:T(1024)}, f32[1536]{0:T(1024)}, f32[1536]{0:T(1024)}, f32[1536]{0:T(1024)}, /*index=5*/f32[1536]...) fusion(f32[512,1536]{1,0:T(8,128)S(1)} %fusion.8, f32[512,1536]{1,0:T(8,128)S(1)} %get-tuple-element.70, ...), kind=kLoop, calls=%fused_computation.25 | loop fusion | flops 21219840 | bytes 6365184 | tf_op jit(solution)/shard_map/reduce_sum | solution.py:76
  142.6 3.8 %multiply_reduce_fusion.20 = (f32[1536]{0:T(1024)}, f32[1536]{0:T(1024)}, f32[1536]{0:T(1024)}, f32[1536]{0:T(1024)}) fusion(f32[512,1536]{1,0:T(8,128)S(1)} %get-tuple-element.70, f32[512,1536]{1,0:T(8,128)S(1)} %fusion.8, f32[512]{0:T(512)S(1)} %bitcast.68, f32[512]{0:T(512)S(1)} %bitcast.71, f32[512]{0:T(512)S(1)} %bitcast.74, f32[512]{0:T(512)S(1)} %bitcast.98), kind=kLoop, calls=%fused_computation.29 | loop fusion | flops 9431040 | bytes 6324224 | tf_op jit(solution)/shard_map/reduce_sum | solution.py:76
  146.5 0.1 broadcast_select_fusion
  146.6 1.3 concatenate.80
  147.9 1.3 concatenate.81
  149.2 1.3 concatenate.82
  150.5 1.3 concatenate.84
  151.8 1.3 concatenate.85
  153.1 1.3 concatenate.86
  154.4 1.3 concatenate.87
  155.7 1.3 concatenate.88
  157.0 1.3 concatenate.89
  158.3 1.3 concatenate.69
  159.6 1.3 concatenate.70
  160.8 1.3 concatenate.71
  162.1 1.3 concatenate.72
  163.4 1.3 concatenate.73
  164.7 1.3 concatenate.74
  166.0 1.3 concatenate.75
  167.3 1.3 concatenate.76
  168.6 1.3 concatenate.83
  170.0 1.3 concatenate.68
  171.3 1.3 concatenate.77
  172.5 1.3 concatenate.78
  173.8 1.3 concatenate.79
  175.2 59.1 %multiply_reduce_fusion = (f32[1536]{0:T(1024)}, f32[512]{0:T(512)S(1)}, f32[512]{0:T(512)S(1)}, f32[]{:T(128)}, f32[512,1536]{1,0:T(8,128)S(1)}) fusion(f32[512,1536]{1,0:T(8,128)} %copy-done.1, f32[512]{0:T(512)S(1)} %add_rsqrt_fusion, f32[512]{0:T(512)S(1)} %broadcast_multiply_fusion.2, f32[1536]{0:T(1024)S(1)} %reshape.206, ...), kind=kLoop, calls=%fused_computation.9 | loop fusion | flops 86504960 | bytes 14430724 | tf_op jit(solution)/shard_map/reduce_sum | solution.py:85
  234.3 2.5 fusion.9
  236.8 1.8 copy.18
  238.6 0.2 select_n.21
  239.2 2.7 fusion.10
  242.1 10.6 %concatenate.100 = f32[544,12,128]{2,0,1:T(8,128)} concatenate(f32[512,12,128]{2,0,1:T(8,128)} %fusion.10, f32[1,12,128]{2,0,1:T(1,128)S(1)} %copy-done.28, f32[1,12,128]{2,0,1:T(1,128)S(1)} %copy-done.19, f32[1,12,128]{2,0,1:T(1,128)S(1)} %copy-done.20, f32[1,12,128]{2,0,1:T(1,128)S(1)} %copy-done.21, f32[1,12,128]{2,0,1:T(1,128)S(1)} %copy-done.22, ...), dimensions={0} | concatenate | bytes 6684672 | tf_op jit(solution)/shard_map/concatenate | solution.py:362
  252.7 2.2 pad.24
  254.9 49.9 %reduce_gradients.1 = f32[544,384]{1,0:T(8,128)S(1)} custom-call(f32[6656,128]{1,0:T(8,128)S(1)} %bitcast.58), custom_call_target="tpu_custom_call" | custom-call | tf_op jit(solution)/shard_map/reduce_gradients/pallas_call | solution.py:298
  304.8 0.9 slice.896
  305.8 0.6 slice.897
  306.4 0.6 slice_reduce_fusion.31
  (152 shorter events, 1.4 us)
Async XLA Ops:
  7.2 1.1 copy-start
  10.3 22.7 %copy-start.45 = (s32[1,1,256]{2,1,0:T(1,128)S(1)}, s32[1,1,256]{2,1,0:T(1,128)}, u32[]{:S(2)}) copy-start(s32[1,1,256]{2,1,0:T(1,128)} %param.10) | copy-start | bytes 3076
  10.3 23.2 %copy-start.43 = (s32[1,1,256]{2,1,0:T(1,128)S(1)}, s32[1,1,256]{2,1,0:T(1,128)}, u32[]{:S(2)}) copy-start(s32[1,1,256]{2,1,0:T(1,128)} %param.11) | copy-start | bytes 3076
  10.3 24.7 %copy-start.44 = (bf16[384]{0:T(512)(128)(2,1)S(1)}, bf16[384]{0:T(512)(128)(2,1)}, u32[]{:S(2)}) copy-start(bf16[384]{0:T(512)(128)(2,1)} %param.14) | copy-start | bytes 2308
  10.3 31.4 %copy-start.32 = (bf16[31,384]{1,0:T(8,128)(2,1)S(1)}, bf16[31,384]{1,0:T(8,128)(2,1)}, u32[]{:S(2)}) copy-start(bf16[31,384]{1,0:T(8,128)(2,1)} %param.15) | copy-start | bytes 71428
  11.6 76.8 %all-to-all-start = ((bf16[128,4,1024]{2,1,0:T(4,128)(2,1)}), bf16[128,4,1024]{2,1,0:T(4,128)(2,1)S(1)}, u32[]{:S(2)}, u32[]{:S(2)}) async-start(bf16[128,4,1024]{2,1,0:T(4,128)(2,1)} %reshape.183), calls=%async_computation | async-start | bytes 2097152 | tf_op jit(solution)/shard_map/all_to_all | solution.py:345
  32.2 57.8 %all-gather.4.cloned.1.call-start = ((), (), s32[]{:S(2)}) async-start(), calls=%async_computation.1 | async-start | bytes 1966080 | tf_op jit(solution)/shard_map/all_gather | solution.py:336
  33.0 0.5 copy-start.41
  49.3 44.9 %copy-start.33 = (f32[512,1]{0,1:T(1,128)}, f32[512,1]{0,1:T(1,128)S(1)}, u32[]{:S(2)}) copy-start(f32[512,1]{0,1:T(1,128)S(1)} %get-tuple-element.75) | copy-start | bytes 6148
  49.3 44.9 %copy-start.34 = (f32[512,1]{0,1:T(1,128)}, f32[512,1]{0,1:T(1,128)S(1)}, u32[]{:S(2)}) copy-start(f32[512,1]{0,1:T(1,128)S(1)} %get-tuple-element.76) | copy-start | bytes 6148
  49.3 44.9 %copy-start.35 = (f32[512,1]{0,1:T(1,128)}, f32[512,1]{0,1:T(1,128)S(1)}, u32[]{:S(2)}) copy-start(f32[512,1]{0,1:T(1,128)S(1)} %get-tuple-element.77) | copy-start | bytes 6148
  49.4 44.9 %copy-start.36 = (f32[512,1]{0,1:T(1,128)}, f32[512,1]{0,1:T(1,128)S(1)}, u32[]{:S(2)}) copy-start(f32[512,1]{0,1:T(1,128)S(1)} %get-tuple-element.78) | copy-start | bytes 6148
  49.4 44.9 %copy-start.37 = (f32[512,1]{0,1:T(1,128)}, f32[512,1]{0,1:T(1,128)S(1)}, u32[]{:S(2)}) copy-start(f32[512,1]{0,1:T(1,128)S(1)} %get-tuple-element.79) | copy-start | bytes 6148
  49.4 44.9 %copy-start.38 = (f32[512,1]{0,1:T(1,128)}, f32[512,1]{0,1:T(1,128)S(1)}, u32[]{:S(2)}) copy-start(f32[512,1]{0,1:T(1,128)S(1)} %get-tuple-element.80) | copy-start | bytes 6148
  49.4 44.9 %copy-start.39 = (f32[512,1]{0,1:T(1,128)}, f32[512,1]{0,1:T(1,128)S(1)}, u32[]{:S(2)}) copy-start(f32[512,1]{0,1:T(1,128)S(1)} %get-tuple-element.81) | copy-start | bytes 6148
  49.4 44.9 %copy-start.40 = (f32[512,1]{0,1:T(1,128)}, f32[512,1]{0,1:T(1,128)S(1)}, u32[]{:S(2)}) copy-start(f32[512,1]{0,1:T(1,128)S(1)} %get-tuple-element.82) | copy-start | bytes 6148
  92.6 1.7 copy-start.1
  93.0 2.1 copy-start.4
  128.0 18.4 %copy-start.3 = (f32[512,1536]{1,0:T(8,128)}, f32[512,1536]{1,0:T(8,128)S(1)}, u32[]{:S(2)}) copy-start(f32[512,1536]{1,0:T(8,128)S(1)} %get-tuple-element.70) | copy-start | bytes 9437188
  142.6 3.9 %copy-start.42 = (pred[256]{0:T(512)(128)(4,1)S(1)}, pred[256]{0:T(512)(128)(4,1)}, u32[]{:S(2)}) copy-start(pred[256]{0:T(512)(128)(4,1)} %copy-done.41) | copy-start | bytes 772
  175.2 59.1 %copy-start.2 = (f32[512,1536]{1,0:T(8,128)S(1)}, f32[512,1536]{1,0:T(8,128)}, u32[]{:S(2)}) copy-start(f32[512,1536]{1,0:T(8,128)} %copy-done.1) | copy-start | bytes 9437188
  236.8 2.0 copy-start.9
  236.8 2.0 copy-start.8
  236.8 2.0 copy-start.7
  236.8 2.1 copy-start.6
  236.8 2.1 copy-start.5
  239.0 2.9 copy-start.10
  239.0 2.9 copy-start.11
  239.0 2.9 copy-start.12
  239.0 2.9 copy-start.13
  239.0 2.9 copy-start.14
  239.0 2.9 copy-start.15
  239.0 2.9 copy-start.16
  239.0 2.9 copy-start.17
  239.0 2.9 copy-start.18
  239.0 2.9 copy-start.19
  239.1 2.9 copy-start.20
  239.1 2.9 copy-start.21
  239.1 2.9 copy-start.22
  239.1 2.9 copy-start.23
  239.1 2.9 copy-start.24
  239.1 2.9 copy-start.25
  239.1 2.9 copy-start.26
  239.1 2.9 copy-start.27
  239.1 2.9 copy-start.28
  239.1 2.9 copy-start.29
  239.2 2.9 copy-start.30
  239.2 2.9 copy-start.31
Sparse Core Ops, SparseCore 0:
  35.2 33.4 all-gather.3

commit v2 on v1

--- a/solution.py
+++ b/solution.py
@@ -18,78 +18,208 @@
 MESH_ID = pl.DeviceIdType.MESH
 
 
-def spread_conv(source_field, kernel_taps, tap_weights):
-    tap_count = kernel_taps.shape[0]
-    half_width = tap_count // 2
-    step_count = source_field.shape[0]
-    padded = jnp.pad(source_field, ((half_width, half_width), (0, 0)))
-    summed = jnp.zeros_like(source_field)
-    for offset in range(tap_count):
-        summed = summed + kernel_taps[offset] * (
-            tap_weights[:, offset : offset + 1] * padded[offset : offset + step_count]
-        )
-    return summed
-
-
-def build_mask(live_steps, utterances, tap_count):
-    half_width = tap_count // 2
-    step_count = live_steps.shape[0]
-    live_pad = jnp.pad(live_steps, (half_width, half_width))
-    utter_pad = jnp.pad(utterances, (half_width, half_width), constant_values=-1)
-    columns = []
-    for offset in range(tap_count):
-        columns.append(
-            live_steps
-            & live_pad[offset : offset + step_count]
-            & (utterances == utter_pad[offset : offset + step_count])
-        )
-    return jnp.stack(columns, axis=1).astype(jnp.float32)
-
-
-def layer_terms(encoded, live_steps, utterances, grad_above, gain, kernel):
-    tap_count = kernel.shape[0]
-    half_width = tap_count // 2
-    step_count = encoded.shape[0]
-    tap_weights = build_mask(live_steps, utterances, tap_count)
-    row_mean = jnp.mean(encoded, axis=1, keepdims=True)
-    centered = encoded - row_mean
-    row_var = jnp.mean(centered * centered, axis=1, keepdims=True)
-    inv_std = lax.rsqrt(row_var + 1e-05)
-    normalized = centered * inv_std
-    gain_f32 = gain.astype(jnp.float32)
-    kernel_taps = kernel.astype(jnp.float32)
-    normed = normalized * gain_f32
-    conv_out = spread_conv(normed, kernel_taps, tap_weights)
-    gate_sig = jax.nn.sigmoid(conv_out)
-    output = encoded + conv_out * gate_sig
-    scale = (encoded.shape[0] * encoded.shape[1]) ** (-0.5)
-    grad_out = (
-        jnp.where(live_steps[:, None], grad_above.astype(jnp.float32), jnp.zeros((), jnp.float32))
-        * scale
-    )
-    device_loss = jnp.sum(output * grad_out)
-    grad_conv = grad_out * (gate_sig * (1.0 + conv_out * (1.0 - gate_sig)))
-    grad_normed = spread_conv(grad_conv, kernel_taps[::-1], tap_weights)
-    padded = jnp.pad(normed, ((half_width, half_width), (0, 0)))
-    grad_taps = jnp.stack(
-        [
-            jnp.sum(
-                grad_conv
-                * tap_weights[:, offset : offset + 1]
-                * padded[offset : offset + step_count],
-                axis=0,
-            )
-            for offset in range(tap_count)
-        ]
-    )
-    grad_scale = jnp.sum(grad_normed * normalized, axis=0)
-    grad_hat = grad_normed * gain_f32
-    grad_x = grad_out + inv_std * (
-        grad_hat
-        - jnp.mean(grad_hat, axis=1, keepdims=True)
-        - normalized * jnp.mean(grad_hat * normalized, axis=1, keepdims=True)
-    )
-    return (device_loss, grad_x.astype(jnp.bfloat16), grad_taps, grad_scale)
+SUB = 8
+SPAN = 42
+HALO = 8
+TAPS = 31
+REACH = TAPS // 2
+BLOCK = 7
+GAP = 8
+ROWS = SPAN * SUB
+
+
+def module_kernel(fr_ref, up_ref, w_ref, gain_ref, taps_ref, out_ref, loss_ref,
+                  x_s, xh_s, go_s, h_s, inv_s, gc_s, sh_s, shx_s, gx_s, ft_s):
+    f32, bf16 = jnp.float32, jnp.bfloat16
+    tiles = gain_ref.shape[0]
+    width = tiles * LANES
+    depth = w_ref.shape[0]
+    scale = (2 * 256 * width) ** (-0.5)
+
+    for h in range(2):
+        frame = fr_ref[:, h * depth : (h + 1) * depth]
+        ft_s[:, h * ROWS : (h + 1) * ROWS] = frame.T
+        x_s[h] = jnp.dot(frame, w_ref[...], preferred_element_type=f32)
+
+    def norm_rows(i, loss):
+        for h in range(2):
+            at = pl.ds(pl.multiple_of(i * 16, 16), 16)
+            xv = x_s[h, at, :]
+            mean = jnp.sum(xv, axis=1, keepdims=True) * (1.0 / width)
+            cen = xv - mean
+            var = jnp.sum(cen * cen, axis=1, keepdims=True) * (1.0 / width)
+            inv = lax.rsqrt(var + 1e-05)
+            inv_s[h, pl.ds(2 * i, 2)] = jnp.broadcast_to(inv, (16, LANES)).reshape(2, SUB, LANES)
+            for c in range(tiles):
+                lanes = slice(c * LANES, (c + 1) * LANES)
+                up = up_ref[pl.ds(pl.multiple_of(h * ROWS + i * 16, 16), 16), lanes]
+                go = up.astype(f32) * scale
+                go_s[c, h, pl.ds(2 * i, 2)] = go.reshape(2, SUB, LANES)
+                xh_s[c, h, pl.ds(HALO + 2 * i, 2)] = (cen[:, lanes] * inv).reshape(2, SUB, LANES)
+                loss = loss + go * xv[:, lanes]
+        return loss
+
+    loss = lax.fori_loop(0, SPAN // 2, norm_rows, jnp.zeros((16, LANES), f32))
+    loss = loss[:SUB] + loss[SUB:]
+
+    sub = lax.broadcasted_iota(jnp.int32, (SUB, LANES), 0)
+
+    def fill_halo(ref):
+        for h in range(2):
+            for j in range(HALO):
+                before = pltpu.roll(ref[h, SPAN + j], 1, 0)
+                ref[h, j] = jnp.where(sub == 0, 0.0, before)
+                after = pltpu.roll(ref[h, HALO + j], SUB - 1, 0)
+                ref[h, HALO + SPAN + j] = jnp.where(sub == SUB - 1, 0.0, after)
+
+    spots = [(h, j) for j in range(BLOCK) for h in range(2)]
+
+    def reach_of(h_in, m):
+        found = []
+        for h, j in spots:
+            d = 2 * (m - j) + h_in - h
+            if -REACH <= d <= REACH:
+                found.append(((h, j), d + REACH))
+        return found
+
+    def conv_block(ref, taps, j0):
+        accs = {}
+        for m in range(-HALO, BLOCK + HALO):
+            for h_in in range(2):
+                uses = reach_of(h_in, m)
+                if not uses:
+                    continue
+                v = ref[h_in, j0 + (HALO + m)]
+                for spot, k in uses:
+                    term = taps[k] * v
+                    accs[spot] = accs[spot] + term if spot in accs else term
+        return accs
+
+    sh_s[...] = jnp.zeros_like(sh_s)
+    shx_s[...] = jnp.zeros_like(shx_s)
+
+    def channel_tile(ct, loss):
+        xh = xh_s.at[ct]
+        fill_halo(xh)
+        gain = jnp.broadcast_to(gain_ref[ct], (SUB, LANES))
+
+        def tap(k):
+            return jnp.broadcast_to(taps_ref[ct, k : k + 1, :], (SUB, LANES))
+
+        def forward(b, loss):
+            j0 = b * BLOCK
+            taps = [tap(k) * gain for k in range(TAPS)]
+            accs = conv_block(xh, taps, j0)
+            for (h, j), c in accs.items():
+                sig = 1.0 / (1.0 + jnp.exp(-c))
+                go = go_s[ct, h, j0 + j]
+                gos = go * sig
+                loss = loss + c * gos
+                gc_s[h, j0 + (HALO + j)] = gos * (1.0 + c * (1.0 - sig))
+            return loss
+
+        loss = lax.fori_loop(0, SPAN // BLOCK, forward, loss)
+        fill_halo(gc_s)
+
+        def backward(b, gg):
+            j0 = b * BLOCK
+            taps = [tap(TAPS - 1 - k) for k in range(TAPS)]
+            accs = conv_block(gc_s, taps, j0)
+            for (h, j), gn in accs.items():
+                v = xh[h, j0 + (HALO + j)]
+                gg = gg + gn * v
+                hv = gn * gain
+                h_s[ct, h, j0 + j] = hv
+                sh_s[h, j0 + j] = sh_s[h, j0 + j] + hv
+                shx_s[h, j0 + j] = shx_s[h, j0 + j] + hv * v
+            return gg
+
+        zero = jnp.zeros((SUB, LANES), f32)
+        gg = lax.fori_loop(0, SPAN // BLOCK, backward, zero)
+
+        def tap_sums(b, sums):
+            j0 = b * BLOCK
+            sums = list(sums)
+            gcs = {(h, j): gc_s[h, j0 + (HALO + j)] for h, j in spots}
+            for m in range(-HALO, BLOCK + HALO):
+                for h_in in range(2):
+                    uses = reach_of(h_in, m)
+                    if not uses:
+                        continue
+                    v = xh[h_in, j0 + (HALO + m)]
+                    for spot, k in uses:
+                        sums[k] = sums[k] + gcs[spot] * v
+            return tuple(sums)
+
+        sums = lax.fori_loop(0, SPAN // BLOCK, tap_sums, (zero,) * TAPS)
+        base = lax.div(ct, 3) * Q_ROWS + lax.rem(ct, 3) * (depth + TAPS + 1) + depth
+        gain_row = gain_ref[ct]
+        tail = [jnp.sum(v, axis=0, keepdims=True) * gain_row for v in sums]
+        tail.append(jnp.sum(gg, axis=0, keepdims=True))
+        out_ref[pl.ds(pl.multiple_of(base, SUB), TAPS + 1), :] = jnp.concatenate(tail, axis=0)
+        return loss
+
+    loss = lax.fori_loop(0, tiles, channel_tile, loss)
+    loss_ref[...] = jnp.sum(loss, keepdims=True)
+
+    def grad_rows(i, carry):
+        for h in range(2):
+            two = pl.ds(2 * i, 2)
+            mh = jnp.sum(sh_s[h, two], axis=2, keepdims=True) * (1.0 / width)
+            mhx = jnp.sum(shx_s[h, two], axis=2, keepdims=True) * (1.0 / width)
+            inv = inv_s[h, two]
+            for c in range(tiles):
+                xv = xh_s[c, h, pl.ds(HALO + 2 * i, 2)]
+                gx = go_s[c, h, two] + inv * (h_s[c, h, two] - mh - xv * mhx)
+                gx_s[pl.ds(pl.multiple_of(h * ROWS + i * 16, 16), 16), c * LANES : (c + 1) * LANES] = (
+                    gx.reshape(16, LANES).astype(bf16)
+                )
+        return carry
+
+    lax.fori_loop(0, SPAN // 2, grad_rows, 0)
+
+    per = 2 * LANES
+    for c in range(0, tiles, 2):
+        gw = jnp.dot(ft_s[...], gx_s[:, c * LANES : c * LANES + per], preferred_element_type=f32)
+        for k in range(2):
+            base = (c + k) // 3 * Q_ROWS + (c + k) % 3 * (depth + TAPS + 1)
+            out_ref[base : base + depth, :] = gw[:, k * LANES : (k + 1) * LANES]
+    used = 3 * (depth + TAPS + 1)
+    for q in range(tiles // 3):
+        out_ref[q * Q_ROWS + used : (q + 1) * Q_ROWS, :] = jnp.zeros((Q_ROWS - used, LANES), f32)
+
+
+def module_terms(frames, above, proj, gain, taps):
+    f32, bf16 = jnp.float32, jnp.bfloat16
+    tiles = proj.shape[1] // LANES
+    depth = proj.shape[0]
+    vm = pl.BlockSpec(memory_space=pltpu.VMEM)
+    gain_tiles = gain.astype(f32).reshape(tiles, 1, LANES)
+    tap_tiles = taps.astype(f32).reshape(TAPS, tiles, LANES).transpose(1, 0, 2)
+    rows = (2, SPAN, SUB, LANES)
+    return pl.pallas_call(
+        module_kernel,
+        out_shape=(
+            jax.ShapeDtypeStruct((tiles // 3 * Q_ROWS, LANES), f32),
+            jax.ShapeDtypeStruct((1, 1), f32),
+        ),
+        in_specs=[vm] * 5,
+        out_specs=(vm, vm),
+        scratch_shapes=[
+            pltpu.VMEM((2, ROWS, tiles * LANES), f32),
+            pltpu.VMEM((tiles, 2, SPAN + 2 * HALO, SUB, LANES), f32),
+            pltpu.VMEM((tiles,) + rows, f32),
+            pltpu.VMEM((tiles,) + rows, f32),
+            pltpu.VMEM(rows, f32),
+            pltpu.VMEM((2, SPAN + 2 * HALO, SUB, LANES), f32),
+            pltpu.VMEM(rows, f32),
+            pltpu.VMEM(rows, f32),
+            pltpu.VMEM((2 * ROWS, tiles * LANES), bf16),
+            pltpu.VMEM((depth, 2 * ROWS), bf16),
+        ],
+        compiler_params=pltpu.CompilerParams(vmem_limit_bytes=56 << 20),
+        name="module_terms",
+    )(frames, above, proj, gain_tiles, tap_tiles)
 
 
 def reduce_kernel(
@@ -338,37 +468,31 @@
         lax.all_gather(norm_gain[None, :], "fsdp", axis=1, tiled=True),
     )
     take_list = take_rows[0, 0]
-    is_live = take_list >= 0
-    safe_index = jnp.maximum(take_list, 0)
-    pair_count = take_list.shape[0]
-    step_width = cache_rows.shape[1] // 2
+    slot = lax.iota(jnp.int32, take_list.shape[0])
+    place = slot + GAP * utt_index[0, 0]
+    order = lax.iota(jnp.int32, ROWS)
+    position = (order % SUB) * SPAN + order // SUB
+    held = (place[None, :] == position[:, None]) & (take_list >= 0)[None, :]
+    source = jnp.max(jnp.where(held, slot[None, :], -1), axis=1)
+    taken = jnp.max(jnp.where(held, take_list[None, :], -1), axis=1)
+    live = source >= 0
+    picked = jnp.maximum(source, 0) * 2
+    steps = jnp.concatenate([picked, picked + 1])
+    above = upstream[0, 0][steps]
+    above = jnp.where(jnp.concatenate([live, live])[:, None], above, jnp.zeros((), above.dtype))
     arrived = lax.all_to_all(outgoing, "dp", split_axis=0, concat_axis=0, tiled=True)
     flat_rows = arrived.reshape(-1, arrived.shape[2])
-    work_rows = jnp.where(is_live[:, None], flat_rows[safe_index], jnp.zeros((), flat_rows.dtype))
-    frames = work_rows.reshape(2 * pair_count, step_width)
-    encoded = jnp.dot(frames, proj_full, preferred_element_type=jnp.float32)
-    live_steps = jnp.repeat(is_live, 2)
-    utterances = jnp.repeat(utt_index[0, 0], 2)
-    device_loss, grad_x, grad_taps, grad_scale = layer_terms(
-        encoded, live_steps, utterances, upstream[0, 0], gain_full[0], taps_full
+    frames = jnp.where(
+        live[:, None], flat_rows[jnp.maximum(taken, 0)], jnp.zeros((), flat_rows.dtype)
     )
-    grad_weight = lax.dot_general(
-        frames, grad_x, (((0,), (0,)), ((), ())), preferred_element_type=jnp.float32
-    )
-    depth, width = grad_weight.shape
-    taps = grad_taps.shape[0]
-    rows = depth + taps + 1
-    quarters = width // in_proj.shape[1]
-    stacked = jnp.concatenate([grad_weight, grad_taps, grad_scale[None, :]], axis=0)
-    tiles = stacked.reshape(rows, width // LANES, LANES).transpose(1, 0, 2)
-    packed = tiles.reshape(quarters, -1, LANES)
-    packed = jnp.pad(packed, ((0, 0), (0, Q_ROWS - packed.shape[1]), (0, 0)))
-    total = reduce_gradients(packed.reshape(-1, LANES), rows, in_proj.shape[1])
+    packed, device_loss = module_terms(frames, above, proj_full, gain_full, taps_full)
+    depth, cols = in_proj.shape
+    total = reduce_gradients(packed, depth + TAPS + 1, cols)
     return (
         total[:depth],
-        total[depth : depth + taps],
-        total[depth + taps],
-        device_loss.reshape(1, 1),
+        total[depth : depth + TAPS],
+        total[depth + TAPS],
+        device_loss,
     )
 
 

time: 315 us -> 204 us (0.65)
  other arithmetic: 115 us -> 6.15 us
  Pallas kernels: 49.9 us -> 98.2 us
  local copies, waits for them, and re-layouts: 54.4 us -> 17.5 us
  waiting for transfers between devices: 39.7 us -> 32.9 us
  matrix products: 5.25 us -> 0 us
    reduce_sum x6 -> x0, other arithmetic: 111 us -> none  [the longest x1 59.1 us: layer_terms(): grad_scale = jnp.sum(grad_normed * normalized, axis=0)]
    pallas_call x0 -> x1, Pallas kernels: none -> 48.2 us  [module_terms(): pl.pallas_call(module_kernel, out_shape=(jax.ShapeDtypeStruct((tiles // 3...]
    concatenate x33 -> x2, local copies, waits for them, and re-layouts: 39.3 us -> 0.01 us  [per_device(): steps = jnp.concatenate([picked, picked + 1])]
    all_to_all x1, waiting for transfers between devices: 39 us -> 32.2 us  [per_device(): lax.all_to_all(outgoing, 'dp', split_axis=0, concat_axis=0, tiled=True)]
    dot_general x2 -> x0, matrix products: 5.25 us -> none  [the longest x1 2.71 us: per_device(): lax.dot_general(frames, grad_x, (((0,), (0,)), ((), ())), preferred_eleme...]
    gather x2, local copies, waits for them, and re-layouts: 1.34 us -> 5.83 us  [the longest x1 3.73 us: per_device(): above = upstream[0, 0][steps]]
    select_n x1 -> x3, other arithmetic: 0.11 us -> 4.3 us  [the longest x1 3.24 us: per_device(): jnp.where(jnp.concatenate([live, live])[:, None], above, jnp.zeros((), ab...]
  transfers between devices with their start and end apart: 2 -> 2, of which waited for: 1 -> 1; matrix products, arithmetic and copies ran while one was open for 1% -> 7% of each run, Pallas kernels for 0% -> 0%
where the time goes in v2:
time: 204 us
  Pallas kernels  98.2 us (48%)
  waiting for transfers between devices  32.9 us (16%)
  starting transfers between devices  21.2 us (10%)
  local copies, waits for them, and re-layouts  17.5 us (9%)
  between operations  14.2 us (7%)
  blocking collectives  13.8 us (7%)
  other arithmetic  6.15 us (3%)
    pallas_call x1, Pallas kernels, reduce_gradients(): pl.pallas_call(reduce_kernel, out_shape=jax.ShapeDtypeStruct((rows, cols)...  49.9 us
    pallas_call x1, Pallas kernels, module_terms(): pl.pallas_call(module_kernel, out_shape=(jax.ShapeDtypeStruct((tiles // 3...  48.2 us
    all_to_all x1, waiting for transfers between devices, per_device(): lax.all_to_all(outgoing, 'dp', split_axis=0, concat_axis=0, tiled=True)  32.2 us
    all_to_all x1, starting transfers between devices, per_device(): lax.all_to_all(outgoing, 'dp', split_axis=0, concat_axis=0, tiled=True)  21.1 us
    all_gather x1, blocking collectives, per_device(): lax.all_gather(conv_kernel, 'fsdp', axis=1, tiled=True)  7.12 us
    all_gather x1, blocking collectives, per_device(): lax.all_gather(norm_gain[None, :], 'fsdp', axis=1, tiled=True)  6.67 us
    gather x2, local copies, waits for them, and re-layouts, per_device(): outgoing = cache_rows[jnp.maximum(wanted, 0)]  5.08 us
  transfers between devices with their start and end apart: 2, of which 1 were waited for; matrix products, arithmetic and copies ran while one was open for 7% of the time, Pallas kernels for 0%

profile of v2, /device:TPU:8, one launch (start us, length us, event | category | flops | bytes accessed | tf_op | source)
XLA Modules:
  0.0 203.9 jit_solution(11685683112309285214)
XLA Ops:
  7.2 0.0 copy-start
  7.2 0.8 broadcast_maximum_fusion
  8.0 0.1 copy.16
  8.1 0.1 reshape.146
  8.2 3.8 %gather_fusion = bf16[512,1024]{1,0:T(8,128)(2,1)S(1)} fusion(bf16[256,1024]{1,0:T(8,128)(2,1)} %bitcast.12, s32[1024]{0:T(1024)S(1)} %pad_clamp_fusion.2), kind=kCustom, calls=%fused_computation | custom fusion | bytes 2099200 | tf_op jit(solution)/shard_map/gather | solution.py:464
  12.1 0.0 copy-start.4
  12.1 0.0 copy-start.3
  12.1 0.0 copy-start.5
  12.1 0.0 copy-start.2
  12.1 1.2 reshape.145
  13.4 21.1 %all-to-all-start = ((bf16[128,4,1024]{2,1,0:T(4,128)(2,1)}), bf16[128,4,1024]{2,1,0:T(4,128)(2,1)}, u32[]{:S(2)}, u32[]{:S(2)}) async-start(bf16[128,4,1024]{2,1,0:T(4,128)(2,1)} %reshape.145), calls=%async_computation | async-start | bytes 2097152 | tf_op jit(solution)/shard_map/all_to_all | solution.py:483
  34.5 0.0 all-gather.4.cloned.1.call-start
  34.5 0.7 all-gather.4.cloned.1.call-update
  35.2 0.0 copy-done.4
  35.2 0.0 copy-done.3
  35.3 0.0 copy-done.5
  35.3 0.3 select_reduce_fusion.1
  35.7 6.7 %all-gather.1 = bf16[4,1,384]{2,1,0:T(2,128)(2,1)S(1)} all-gather(bf16[1,1,384]{2,1,0:T(2,128)(2,1)S(1)} %reshape.175), channel_id=2, replica_groups=mesh['dp'=128,'fsdp'=4] {'fsdp'}, dimensions={0}, use_global_device_ids=true | all-gather | bytes 3840 | tf_op jit(solution)/shard_map/all_gather | solution.py:468
  42.3 0.6 convert.3.gain_ref
  42.9 0.0 copy-done.2
  42.9 7.1 %all_gather.11 = bf16[31,1536]{1,0:T(8,128)(2,1)S(1)} all-gather(bf16[31,384]{1,0:T(8,128)(2,1)S(1)} %copy-done.2), channel_id=1, replica_groups=mesh['dp'=128,'fsdp'=4] {'fsdp'}, dimensions={1}, use_global_device_ids=true | all-gather | bytes 119040 | tf_op jit(solution)/shard_map/all_gather | solution.py:467
  50.1 0.1 reshape.143
  50.2 0.8 copy.19
  50.9 0.1 fusion.4
  51.0 0.0 copy-done
  51.0 3.7 %gather_fusion.2 = bf16[672,1536]{1,0:T(8,128)(2,1)} fusion(bf16[512,1536]{1,0:T(8,128)(2,1)S(1)} %bitcast.11, s32[1024]{0:T(1024)S(1)} %pad_clamp_fusion), kind=kCustom, calls=%fused_computation.2 | custom fusion | bytes 4131456 | tf_op jit(solution)/shard_map/gather | solution.py:481
  54.8 0.1 pad_add_fusion
  54.8 3.2 %broadcast_select_fusion.up_ref = bf16[672,1536]{1,0:T(8,128)(2,1)} fusion(bf16[672,1536]{1,0:T(8,128)(2,1)} %gather_fusion.2, pred[672]{0:T(1024)(128)(4,1)S(1)} %pad_add_fusion), kind=kLoop, calls=%fused_computation.3 | loop fusion | flops 1032192 | bytes 4129440 | tf_op jit(solution)/shard_map/jit(_where)/select_n | solution.py:482
  58.1 32.2 %all-to-all-done = bf16[128,4,1024]{2,1,0:T(4,128)(2,1)} async-done(((bf16[128,4,1024]{2,1,0:T(4,128)(2,1)}), bf16[128,4,1024]{2,1,0:T(4,128)(2,1)}, u32[]{:S(2)}, u32[]{:S(2)}) %all-to-all-start) | async-done | bytes 1048608 | tf_op jit(solution)/shard_map/all_to_all | solution.py:483
  90.3 1.3 reshape.137
  91.6 2.1 %gather_fusion.1 = bf16[336,1024]{1,0:T(8,128)(2,1)S(1)} fusion(bf16[512,1024]{1,0:T(8,128)(2,1)S(1)} %reshape.137, s32[1024]{0:T(1024)S(1)} %pad_clamp_fusion.1), kind=kCustom, calls=%fused_computation.1 | custom fusion | bytes 1377600 | tf_op jit(solution)/shard_map/gather | solution.py:486
  93.8 1.0 broadcast_select_fusion.1.fr_ref
  94.7 0.0 all-gather.4.cloned.1.call-done.w_ref
  94.7 48.2 %module_terms.1 = (f32[6656,128]{1,0:T(8,128)}, f32[1,1]{1,0:T(1,128)}) custom-call(bf16[336,1024]{1,0:T(8,128)(2,1)} %broadcast_select_fusion.1.fr_ref, bf16[672,1536]{1,0:T(8,128)(2,1)} %broadcast_select_fusion.up_ref, bf16[512,1536]{1,0:T(8,128)(2,1)} %all-gather.4.cloned.1.call-done.w_ref, f32[12,1,128]{2,1,0:T(1,128)} %convert.3.gain_ref, ...), custom_call_target="tpu_custom_call" | custom-call | tf_op jit(solution)/shard_map/module_terms/pallas_call | solution.py:200
  143.0 0.0 copy-start.1
  143.0 2.0 copy-done.1
  144.9 49.9 %reduce_gradients.1 = f32[544,384]{1,0:T(8,128)S(1)} custom-call(f32[6656,128]{1,0:T(8,128)S(1)} %copy-done.1), custom_call_target="tpu_custom_call" | custom-call | tf_op jit(solution)/shard_map/reduce_gradients/pallas_call | solution.py:428
  194.9 0.6 slice_reduce_fusion
  195.5 0.6 slice.10
  196.1 0.9 slice.9
  (13 shorter events, 0.1 us)
Async XLA Ops:
  7.2 43.8 %copy-start = (bf16[1,1,512,1536]{3,2,1,0:T(8,128)(2,1)S(1)}, bf16[1,1,512,1536]{3,2,1,0:T(8,128)(2,1)}, u32[]{:S(2)}) copy-start(bf16[1,1,512,1536]{3,2,1,0:T(8,128)(2,1)} %param.12) | copy-start | bytes 4718596
  12.1 23.2 %copy-start.4 = (bf16[384]{0:T(512)(128)(2,1)S(1)}, bf16[384]{0:T(512)(128)(2,1)}, u32[]{:S(2)}) copy-start(bf16[384]{0:T(512)(128)(2,1)} %param.14) | copy-start | bytes 2308
  12.1 23.2 %copy-start.3 = (s32[1,1,256]{2,1,0:T(1,128)S(1)}, s32[1,1,256]{2,1,0:T(1,128)}, u32[]{:S(2)}) copy-start(s32[1,1,256]{2,1,0:T(1,128)} %param.10) | copy-start | bytes 3076
  12.1 23.2 %copy-start.5 = (s32[1,1,256]{2,1,0:T(1,128)S(1)}, s32[1,1,256]{2,1,0:T(1,128)}, u32[]{:S(2)}) copy-start(s32[1,1,256]{2,1,0:T(1,128)} %param.11) | copy-start | bytes 3076
  12.1 30.8 %copy-start.2 = (bf16[31,384]{1,0:T(8,128)(2,1)S(1)}, bf16[31,384]{1,0:T(8,128)(2,1)}, u32[]{:S(2)}) copy-start(bf16[31,384]{1,0:T(8,128)(2,1)} %param.15) | copy-start | bytes 71428
  13.4 76.9 %all-to-all-start = ((bf16[128,4,1024]{2,1,0:T(4,128)(2,1)}), bf16[128,4,1024]{2,1,0:T(4,128)(2,1)}, u32[]{:S(2)}, u32[]{:S(2)}) async-start(bf16[128,4,1024]{2,1,0:T(4,128)(2,1)} %reshape.145), calls=%async_computation | async-start | bytes 2097152 | tf_op jit(solution)/shard_map/all_to_all | solution.py:483
  34.5 60.2 %all-gather.4.cloned.1.call-start = ((), (), s32[]{:S(2)}) async-start(), calls=%async_computation.1 | async-start | bytes 1966080 | tf_op jit(solution)/shard_map/all_gather | solution.py:466
  143.0 2.0 copy-start.1
Sparse Core Ops, SparseCore 0:
  37.4 33.4 all-gather.3

commit v3 on v2

--- a/solution.py
+++ b/solution.py
@@ -37,7 +37,7 @@
     scale = (2 * 256 * width) ** (-0.5)
 
     for h in range(2):
-        frame = fr_ref[:, h * depth : (h + 1) * depth]
+        frame = fr_ref[h * ROWS : (h + 1) * ROWS, :]
         ft_s[:, h * ROWS : (h + 1) * ROWS] = frame.T
         x_s[h] = jnp.dot(frame, w_ref[...], preferred_element_type=f32)
 
@@ -189,13 +189,11 @@
         out_ref[q * Q_ROWS + used : (q + 1) * Q_ROWS, :] = jnp.zeros((Q_ROWS - used, LANES), f32)
 
 
-def module_terms(frames, above, proj, gain, taps):
+def module_terms(frames, above, proj, tap_tiles, gain_tiles):
     f32, bf16 = jnp.float32, jnp.bfloat16
     tiles = proj.shape[1] // LANES
     depth = proj.shape[0]
     vm = pl.BlockSpec(memory_space=pltpu.VMEM)
-    gain_tiles = gain.astype(f32).reshape(tiles, 1, LANES)
-    tap_tiles = taps.astype(f32).reshape(TAPS, tiles, LANES).transpose(1, 0, 2)
     rows = (2, SPAN, SUB, LANES)
     return pl.pallas_call(
         module_kernel,
@@ -220,6 +218,201 @@
         compiler_params=pltpu.CompilerParams(vmem_limit_bytes=56 << 20),
         name="module_terms",
     )(frames, above, proj, gain_tiles, tap_tiles)
+
+
+def exchange_kernel(
+    cache_ref, want_ref, take_ref, utt_ref, tpos_ref, up_ref, w_ref, taps_ref, gain_ref,
+    fr_ref, above_ref, proj_ref, tapt_ref, gaint_ref,
+    pick_s, send_s, arr_s, taps_s, gain_s,
+    row_s, row_r, par_s, par_r,
+):
+    f32, bf16 = jnp.float32, jnp.bfloat16
+    peers = arr_s.shape[0]
+    members = proj_ref.shape[1] // w_ref.shape[1]
+    cols = w_ref.shape[1]
+    p = lax.axis_index("dp")
+    f = lax.axis_index("fsdp")
+
+    def peer(o):
+        return lax.rem(p + o, peers)
+
+    barrier = pltpu.get_barrier_semaphore()
+
+    def greet(o, carry):
+        pl.semaphore_signal(barrier, inc=1, device_id=(peer(o), f), device_id_type=MESH_ID)
+        return carry
+
+    lax.fori_loop(1, peers, greet, 0)
+    for o in range(1, members):
+        pl.semaphore_signal(
+            barrier, inc=1, device_id=(p, lax.rem(f + o, members)), device_id_type=MESH_ID
+        )
+
+    count, width = cache_ref.shape
+    half = width // 2
+    want = jnp.concatenate([want_ref[...], want_ref[...]], axis=0)
+    cache_ids = lax.broadcasted_iota(jnp.int32, (SUB, count), 1)
+    for d in range(0, peers, 2):
+        two = [
+            (jnp.broadcast_to(want[:, d + k : d + k + 1], (SUB, count)) == cache_ids).astype(f32)
+            for k in range(2)
+        ]
+        pick_s[d * SUB : (d + 2) * SUB, :count] = jnp.concatenate(two, axis=0).astype(bf16)
+    step = 256
+    first = lax.broadcasted_iota(jnp.int32, (step, half), 0) % SUB < SUB // 2
+    for r in range(0, peers * SUB, step):
+        rows = jnp.dot(pick_s[r : r + step, :count], cache_ref[...], preferred_element_type=f32)
+        rows = jnp.where(first, rows[:, :half], rows[:, half:])
+        send_s[r // SUB : (r + step) // SUB] = rows.reshape(step // SUB, SUB, half).astype(bf16)
+
+    pl.semaphore_wait(barrier, peers - 1 + members - 1)
+
+    def row_copy(o):
+        return pltpu.make_async_remote_copy(
+            src_ref=send_s.at[peer(o)],
+            dst_ref=arr_s.at[p],
+            send_sem=row_s,
+            recv_sem=row_r,
+            device_id=(peer(o), f),
+            device_id_type=MESH_ID,
+        )
+
+    def param_copies(o):
+        lanes = pl.ds(pl.multiple_of(f * cols, LANES), cols)
+        pairs = [(w_ref, proj_ref), (taps_ref, taps_s), (gain_ref, gain_s)]
+        return [
+            pltpu.make_async_remote_copy(
+                src_ref=src,
+                dst_ref=dst.at[:, lanes],
+                send_sem=par_s.at[3 * (o - 1) + i],
+                recv_sem=par_r.at[3 * (o - 1) + i],
+                device_id=(p, lax.rem(f + o, members)),
+                device_id_type=MESH_ID,
+            )
+            for i, (src, dst) in enumerate(pairs)
+        ]
+
+    row_copy(peers // 2).start()
+
+    def start_rows(i, carry):
+        o = peers // 2 - i
+        row_copy(o).start()
+        row_copy(peers - o).start()
+        return carry
+
+    lax.fori_loop(1, peers // 2, start_rows, 0)
+    for o in range(1, members):
+        for copy in param_copies(o):
+            copy.start()
+    arr_s[p] = send_s[p]
+    own = pl.ds(pl.multiple_of(f * cols, LANES), cols)
+    proj_ref[:, own] = w_ref[...]
+    taps_s[:, own] = taps_ref[...]
+    gain_s[:, own] = gain_ref[...]
+
+    sub = lax.broadcasted_iota(jnp.int32, (SUB, 1), 0)
+    steps = tpos_ref.shape[1]
+    slots = take_ref.shape[1]
+    place = lax.broadcasted_iota(jnp.int32, (1, slots), 1) + GAP * utt_ref[...]
+    place = jnp.broadcast_to(place, (SUB, slots))
+    take = jnp.broadcast_to(take_ref[...], (SUB, slots))
+    tpos = jnp.broadcast_to(tpos_ref[...], (SUB, steps))
+    for h in range(2):
+        for j in range(0, SPAN, 2):
+            two = [
+                (tpos == 2 * (sub * SPAN + (j + k)) + h).astype(f32) for k in range(2)
+            ]
+            row = h * ROWS + j * SUB
+            pick_s[row : row + 2 * SUB, :steps] = jnp.concatenate(two, axis=0).astype(bf16)
+    for r in range(0, 2 * ROWS, ROWS // 2):
+        above_ref[r : r + ROWS // 2, :] = jnp.dot(
+            pick_s[r : r + ROWS // 2, :steps], up_ref[...], preferred_element_type=f32
+        ).astype(bf16)
+    arrived = lax.broadcasted_iota(jnp.int32, (SUB, peers * SUB), 1)
+    for j in range(0, SPAN, 2):
+        twos = ([], [])
+        for k in range(2):
+            held = place == sub * SPAN + (j + k)
+            taken = jnp.max(jnp.where(held, take, -1), axis=1, keepdims=True)
+            taken = jnp.where(taken < 0, -SUB, taken + taken // 4 * 4)
+            for h in range(2):
+                twos[h].append((jnp.broadcast_to(taken + 4 * h, arrived.shape) == arrived).astype(f32))
+        for h in range(2):
+            row = h * ROWS + j * SUB
+            pick_s[row : row + 2 * SUB, :] = jnp.concatenate(twos[h], axis=0).astype(bf16)
+
+    for o in range(1, members):
+        for copy in param_copies(o):
+            copy.wait_recv()
+    tiles = gaint_ref.shape[0]
+    for c in range(tiles):
+        lanes = slice(c * LANES, (c + 1) * LANES)
+        tapt_ref[c] = taps_s[:, lanes].astype(f32)
+        gaint_ref[c] = gain_s[:, lanes].astype(f32)
+
+    whole = pltpu.make_async_remote_copy(
+        src_ref=send_s.at[pl.ds(0, peers - 1)],
+        dst_ref=arr_s.at[pl.ds(0, peers - 1)],
+        send_sem=row_s,
+        recv_sem=row_r,
+        device_id=(peer(1), f),
+        device_id_type=MESH_ID,
+    )
+    whole.wait_recv()
+    table = arr_s[...].astype(f32).reshape(peers * SUB, half).astype(bf16)
+    for h in range(2):
+        rows = slice(h * ROWS, (h + 1) * ROWS)
+        fr_ref[rows, :] = jnp.dot(pick_s[rows, :], table, preferred_element_type=f32).astype(bf16)
+    whole.wait_send()
+    for o in range(1, members):
+        for copy in param_copies(o):
+            copy.wait_send()
+
+
+def exchange(cache_rows, wanted, take, utt, upstream, in_proj, taps, gain, members):
+    f32, bf16, i32 = jnp.float32, jnp.bfloat16, jnp.int32
+    peers = wanted.shape[0]
+    slots = take.shape[0]
+    step = lax.iota(i32, 2 * slots)
+    place = lax.iota(i32, slots) + GAP * utt
+    tpos = jnp.where(
+        jnp.repeat(take, 2) >= 0, 2 * jnp.repeat(place, 2) + step % 2, -1
+    )
+    depth, cols = in_proj.shape
+    width = cols * members
+    tiles = width // LANES
+    half = cache_rows.shape[1] // 2
+    vm = pl.BlockSpec(memory_space=pltpu.VMEM)
+    dma = pltpu.SemaphoreType.DMA
+    shape = jax.ShapeDtypeStruct
+    return pl.pallas_call(
+        exchange_kernel,
+        out_shape=(
+            shape((2 * ROWS, half), bf16),
+            shape((2 * ROWS, width), bf16),
+            shape((depth, width), bf16),
+            shape((tiles, TAPS, LANES), f32),
+            shape((tiles, 1, LANES), f32),
+        ),
+        in_specs=[vm] * 9,
+        out_specs=(vm,) * 5,
+        scratch_shapes=[
+            pltpu.VMEM((max(2 * ROWS, peers * SUB), peers * SUB), bf16),
+            pltpu.VMEM((peers, SUB, half), bf16),
+            pltpu.VMEM((peers, SUB, half), bf16),
+            pltpu.VMEM((TAPS, width), bf16),
+            pltpu.VMEM((1, width), bf16),
+            dma, dma,
+            dma((3 * (members - 1),)), dma((3 * (members - 1),)),
+        ],
+        compiler_params=pltpu.CompilerParams(
+            collective_id=1, has_side_effects=True, vmem_limit_bytes=40 << 20
+        ),
+        name="exchange",
+    )(
+        cache_rows, wanted.T, take[None, :], utt[None, :], tpos[None, :], upstream,
+        in_proj, taps, gain[None, :],
+    )
 
 
 def reduce_kernel(
@@ -458,34 +651,14 @@
     )(packed)
 
 
-def per_device(cached, send_rows, take_rows, utt_index, upstream, in_proj, norm_gain, conv_kernel):
-    cache_rows = cached[0, 0]
-    wanted = send_rows[0, 0]
-    outgoing = cache_rows[jnp.maximum(wanted, 0)]
-    proj_full, taps_full, gain_full = (
-        lax.all_gather(in_proj, "fsdp", axis=1, tiled=True),
-        lax.all_gather(conv_kernel, "fsdp", axis=1, tiled=True),
-        lax.all_gather(norm_gain[None, :], "fsdp", axis=1, tiled=True),
+def per_device(
+    members, cached, send_rows, take_rows, utt_index, upstream, in_proj, norm_gain, conv_kernel
+):
+    moved = exchange(
+        cached[0, 0], send_rows[0, 0], take_rows[0, 0], utt_index[0, 0], upstream[0, 0],
+        in_proj, conv_kernel, norm_gain, members,
     )
-    take_list = take_rows[0, 0]
-    slot = lax.iota(jnp.int32, take_list.shape[0])
-    place = slot + GAP * utt_index[0, 0]
-    order = lax.iota(jnp.int32, ROWS)
-    position = (order % SUB) * SPAN + order // SUB
-    held = (place[None, :] == position[:, None]) & (take_list >= 0)[None, :]
-    source = jnp.max(jnp.where(held, slot[None, :], -1), axis=1)
-    taken = jnp.max(jnp.where(held, take_list[None, :], -1), axis=1)
-    live = source >= 0
-    picked = jnp.maximum(source, 0) * 2
-    steps = jnp.concatenate([picked, picked + 1])
-    above = upstream[0, 0][steps]
-    above = jnp.where(jnp.concatenate([live, live])[:, None], above, jnp.zeros((), above.dtype))
-    arrived = lax.all_to_all(outgoing, "dp", split_axis=0, concat_axis=0, tiled=True)
-    flat_rows = arrived.reshape(-1, arrived.shape[2])
-    frames = jnp.where(
-        live[:, None], flat_rows[jnp.maximum(taken, 0)], jnp.zeros((), flat_rows.dtype)
-    )
-    packed, device_loss = module_terms(frames, above, proj_full, gain_full, taps_full)
+    packed, device_loss = module_terms(*moved)
     depth, cols = in_proj.shape
     total = reduce_gradients(packed, depth + TAPS + 1, cols)
     return (
@@ -508,7 +681,7 @@
         P(None, "fsdp"),
     )
     return jax.shard_map(
-        per_device,
+        functools.partial(per_device, mesh.shape["fsdp"]),
         mesh=mesh,
         in_specs=placed,
         out_specs=(P(None, "fsdp"), P(None, "fsdp"), P("fsdp"), P("dp", "fsdp")),

time: 204 us -> 187 us (0.917)
  the two profiles are of different devices: /device:TPU:8 before, /device:TPU:2 now
where the time goes in v3:
time: 187 us; the launch traced here: 186 us
  Pallas kernels  168 us (90%)
  local copies, waits for them, and re-layouts  16.1 us (9%)
    pallas_call x1, Pallas kernels, exchange(): pl.pallas_call(exchange_kernel, out_shape=(shape((2 * ROWS, half), bf16),...  66.3 us
    pallas_call x1, Pallas kernels, reduce_gradients(): pl.pallas_call(reduce_kernel, out_shape=jax.ShapeDtypeStruct((rows, cols)...  53.6 us
    pallas_call x1, Pallas kernels, module_terms(): pl.pallas_call(module_kernel, out_shape=(jax.ShapeDtypeStruct((tiles // 3...  48.2 us
    unnamed x26, local copies, waits for them, and re-layouts  12.8 us

profile of v3, /device:TPU:2, one launch (start us, length us, event | category | flops | bytes accessed | tf_op | source)
XLA Modules:
  0.0 186.3 jit_solution(9572402316329123523)
XLA Ops:
  0.6 0.7 compare_reduce_fusion
  1.3 0.7 broadcast_multiply_fusion
  2.0 0.7 broadcast_in_dim.17.gain_ref
  2.7 0.1 broadcast_in_dim.14
  2.8 0.2 ge.25
  3.0 0.1 broadcast_in_dim.15
  3.1 0.1 mul.33
  3.2 0.0 copy-start.2
  3.2 1.4 copy-done.2
  4.6 0.0 copy-start.5
  4.6 1.0 copy-done.5
  5.7 0.0 copy-start.6
  5.7 1.0 copy-done.6
  6.7 0.0 copy-start.8
  6.7 0.7 copy-done.8
  7.4 0.0 copy-start.10
  7.4 0.7 copy-done.10
  8.1 0.0 copy-start.11
  8.1 0.7 copy-done.11
  8.8 0.0 copy-start.12
  8.8 0.7 copy-done.12
  9.4 66.3 %exchange.1 = (bf16[672,512]{1,0:T(8,128)(2,1)S(1)}, bf16[672,1536]{1,0:T(8,128)(2,1)S(1)}, bf16[512,1536]{1,0:T(8,128)(2,1)S(1)}, f32[12,31,128]{2,1,0:T(8,128)S(1)}, f32[12,1,128]{2,1,0:T(1,128)S(1)}) custom-call(bf16[256,1024]{1,0:T(8,128)(2,1)S(1)} %bitcast.9, s32[4,128]{1,0:T(4,128)S(1)} %bitcast.11, s32[1,256]{1,0:T(1,128)S(1)} %bitcast.12, ...), custom_call_target="tpu_custom_call" | custom-call | tf_op jit(solution)/shard_map/exchange/pallas_call | solution.py:388
  75.8 0.0 copy-start.1
  75.8 1.3 copy-done.1
  77.1 0.0 copy-start.3
  77.1 1.2 copy-done.3
  78.3 0.0 copy-start.4
  78.3 0.8 copy-done.4
  79.1 0.0 copy-start.7
  79.1 0.7 copy-done.7
  79.8 0.0 copy-start.9
  79.8 0.6 copy-done.9
  80.4 48.2 %module_terms.1 = (f32[6656,128]{1,0:T(8,128)}, f32[1,1]{1,0:T(1,128)}) custom-call(bf16[672,512]{1,0:T(8,128)(2,1)} %copy-done.4, bf16[672,1536]{1,0:T(8,128)(2,1)} %copy-done.1, bf16[512,1536]{1,0:T(8,128)(2,1)} %copy-done.3, f32[12,1,128]{2,1,0:T(1,128)} %copy-done.9, f32[12,31,128]{2,1,0:T(8,128)} %copy-done.7), custom_call_target="tpu_custom_call" | custom-call | tf_op jit(solution)/shard_map/module_terms/pallas_call | solution.py:198
  128.6 0.0 copy-start
  128.6 2.0 %copy-done = f32[6656,128]{1,0:T(8,128)S(1)} copy-done((f32[6656,128]{1,0:T(8,128)S(1)}, f32[6656,128]{1,0:T(8,128)}, u32[]{:S(2)}) %copy-start) | copy-done | bytes 3407896
  130.5 53.6 %reduce_gradients.1 = f32[544,384]{1,0:T(8,128)S(1)} custom-call(f32[6656,128]{1,0:T(8,128)S(1)} %copy-done), custom_call_target="tpu_custom_call" | custom-call | tf_op jit(solution)/shard_map/reduce_gradients/pallas_call | solution.py:621
  184.1 0.6 slice_reduce_fusion
  184.7 0.6 slice.10
  185.4 0.9 slice.9
  (2 shorter events, 0.0 us)
Async XLA Ops:
  3.2 1.4 copy-start.2
  4.6 1.0 copy-start.5
  5.7 1.0 copy-start.6
  6.7 0.7 copy-start.8
  7.4 0.7 copy-start.10
  8.1 0.7 copy-start.11
  8.8 0.7 copy-start.12
  75.8 1.3 copy-start.1
  77.1 1.2 copy-start.3
  78.3 0.8 copy-start.4
  79.1 0.7 copy-start.7
  79.8 0.6 copy-start.9
  128.6 2.0 %copy-start = (f32[6656,128]{1,0:T(8,128)S(1)}, f32[6656,128]{1,0:T(8,128)}, u32[]{:S(2)}) copy-start(f32[6656,128]{1,0:T(8,128)} %get-tuple-element.16.g_ref) | copy-start | bytes 10223620

commit v4 on v3

--- a/solution.py
+++ b/solution.py
@@ -23,14 +23,29 @@
 HALO = 8
 TAPS = 31
 REACH = TAPS // 2
-BLOCK = 7
+BLOCK = 14
 GAP = 8
 ROWS = SPAN * SUB
 
 
-def module_kernel(fr_ref, up_ref, w_ref, gain_ref, taps_ref, out_ref, loss_ref,
-                  x_s, xh_s, go_s, h_s, inv_s, gc_s, sh_s, shx_s, gx_s, ft_s):
+def module_kernel(fr_hbm, up_hbm, w_hbm, gain_hbm, taps_hbm, out_ref, loss_ref,
+                  x_s, xh_s, go_s, h_s, inv_s, gc_s, sh_s, shx_s, gx_s, ft_s,
+                  tb_s, cx_s, cg_s, p_s, q_s,
+                  fr_ref, up_ref, w_ref, gain_ref, taps_ref, in_sem):
     f32, bf16 = jnp.float32, jnp.bfloat16
+    loads = [
+        pltpu.make_async_copy(src, dst, in_sem.at[i])
+        for i, (src, dst) in enumerate(
+            [
+                (w_hbm, w_ref), (fr_hbm, fr_ref), (up_hbm, up_ref),
+                (gain_hbm, gain_ref), (taps_hbm, taps_ref),
+            ]
+        )
+    ]
+    for load in loads:
+        load.start()
+    loads[0].wait()
+    loads[1].wait()
     tiles = gain_ref.shape[0]
     width = tiles * LANES
     depth = w_ref.shape[0]
@@ -40,6 +55,9 @@
         frame = fr_ref[h * ROWS : (h + 1) * ROWS, :]
         ft_s[:, h * ROWS : (h + 1) * ROWS] = frame.T
         x_s[h] = jnp.dot(frame, w_ref[...], preferred_element_type=f32)
+
+    for load in loads[2:]:
+        load.wait()
 
     def norm_rows(i, loss):
         for h in range(2):
@@ -72,28 +90,57 @@
                 after = pltpu.roll(ref[h, HALO + j], SUB - 1, 0)
                 ref[h, HALO + SPAN + j] = jnp.where(sub == SUB - 1, 0.0, after)
 
-    spots = [(h, j) for j in range(BLOCK) for h in range(2)]
-
-    def reach_of(h_in, m):
-        found = []
-        for h, j in spots:
-            d = 2 * (m - j) + h_in - h
-            if -REACH <= d <= REACH:
-                found.append(((h, j), d + REACH))
-        return found
-
-    def conv_block(ref, taps, j0):
+    evens = range(-(REACH // 2), REACH // 2 + 1)
+    odds = range(-(REACH // 2) - 1, REACH // 2 + 1)
+
+    def even_tap(m):
+        return 2 * m + REACH
+
+    def odd_tap(m):
+        return 2 * m + 1 + REACH
+
+    def slide(get, taps, j0):
         accs = {}
-        for m in range(-HALO, BLOCK + HALO):
-            for h_in in range(2):
-                uses = reach_of(h_in, m)
-                if not uses:
-                    continue
-                v = ref[h_in, j0 + (HALO + m)]
-                for spot, k in uses:
-                    term = taps[k] * v
-                    accs[spot] = accs[spot] + term if spot in accs else term
+        for i in range(min(taps), BLOCK + max(taps)):
+            v = get(j0 + (HALO + i))
+            for j in range(BLOCK):
+                if i - j in taps:
+                    term = taps[i - j] * v
+                    accs[j] = accs[j] + term if j in accs else term
         return accs
+
+    def cross_sums(ref, cross):
+        for j in range(2 * HALO + SPAN - 1):
+            cross[j] = ref[1, j] + ref[0, j + 1]
+
+    def conv(ref, cross, tap, use, carry):
+        def parts(b, c):
+            j0 = b * BLOCK
+            own = slide(lambda j: ref[0, j], {m: tap(even_tap(m)) for m in evens}, j0)
+            for j, v in own.items():
+                p_s[j0 + j] = v
+            own = slide(lambda j: ref[1, j], {m: tap(odd_tap(m)) for m in odds}, j0)
+            for j, v in own.items():
+                q_s[j0 + j] = v
+            return c
+
+        lax.fori_loop(0, SPAN // BLOCK, parts, 0)
+        cross_sums(ref, cross)
+        p_s[SPAN] = jnp.where(sub == SUB - 1, 0.0, pltpu.roll(p_s[0], SUB - 1, 0))
+
+        def joined(b, carry):
+            j0 = b * BLOCK
+            both = {}
+            for m in odds:
+                both[m] = tap(odd_tap(m)) + tap(even_tap(m)) if m in evens else tap(odd_tap(m))
+            third = slide(lambda j: cross[j], both, j0)
+            for j in range(BLOCK):
+                q = q_s[j0 + j]
+                carry = use(0, j0 + j, p_s[j0 + j] + q, carry)
+                carry = use(1, j0 + j, third[j] - (p_s[j0 + (j + 1)] + q), carry)
+            return carry
+
+        return lax.fori_loop(0, SPAN // BLOCK, joined, carry)
 
     sh_s[...] = jnp.zeros_like(sh_s)
     shx_s[...] = jnp.zeros_like(shx_s)
@@ -102,59 +149,60 @@
         xh = xh_s.at[ct]
         fill_halo(xh)
         gain = jnp.broadcast_to(gain_ref[ct], (SUB, LANES))
-
-        def tap(k):
-            return jnp.broadcast_to(taps_ref[ct, k : k + 1, :], (SUB, LANES))
-
-        def forward(b, loss):
-            j0 = b * BLOCK
-            taps = [tap(k) * gain for k in range(TAPS)]
-            accs = conv_block(xh, taps, j0)
-            for (h, j), c in accs.items():
-                sig = 1.0 / (1.0 + jnp.exp(-c))
-                go = go_s[ct, h, j0 + j]
-                gos = go * sig
-                loss = loss + c * gos
-                gc_s[h, j0 + (HALO + j)] = gos * (1.0 + c * (1.0 - sig))
-            return loss
-
-        loss = lax.fori_loop(0, SPAN // BLOCK, forward, loss)
+        for k in range(TAPS):
+            tap = jnp.broadcast_to(taps_ref[ct, k : k + 1, :], (SUB, LANES))
+            tb_s[0, k] = tap * gain
+            tb_s[1, TAPS - 1 - k] = tap
+
+        def forward(h, j, c, loss):
+            sig = 1.0 / (1.0 + jnp.exp(-c))
+            gos = go_s[ct, h, j] * sig
+            gc_s[h, j + HALO] = gos * (1.0 + c * (1.0 - sig))
+            return loss + c * gos
+
+        loss = conv(xh, cx_s, lambda k: tb_s[0, k], forward, loss)
         fill_halo(gc_s)
 
-        def backward(b, gg):
-            j0 = b * BLOCK
-            taps = [tap(TAPS - 1 - k) for k in range(TAPS)]
-            accs = conv_block(gc_s, taps, j0)
-            for (h, j), gn in accs.items():
-                v = xh[h, j0 + (HALO + j)]
-                gg = gg + gn * v
-                hv = gn * gain
-                h_s[ct, h, j0 + j] = hv
-                sh_s[h, j0 + j] = sh_s[h, j0 + j] + hv
-                shx_s[h, j0 + j] = shx_s[h, j0 + j] + hv * v
-            return gg
+        def backward(h, j, gn, gg):
+            v = xh[h, j + HALO]
+            hv = gn * gain
+            h_s[ct, h, j] = hv
+            sh_s[h, j] = sh_s[h, j] + hv
+            shx_s[h, j] = shx_s[h, j] + hv * v
+            return gg + gn * v
 
         zero = jnp.zeros((SUB, LANES), f32)
-        gg = lax.fori_loop(0, SPAN // BLOCK, backward, zero)
-
-        def tap_sums(b, sums):
-            j0 = b * BLOCK
-            sums = list(sums)
-            gcs = {(h, j): gc_s[h, j0 + (HALO + j)] for h, j in spots}
-            for m in range(-HALO, BLOCK + HALO):
-                for h_in in range(2):
-                    uses = reach_of(h_in, m)
-                    if not uses:
-                        continue
-                    v = xh[h_in, j0 + (HALO + m)]
-                    for spot, k in uses:
-                        sums[k] = sums[k] + gcs[spot] * v
-            return tuple(sums)
-
-        sums = lax.fori_loop(0, SPAN // BLOCK, tap_sums, (zero,) * TAPS)
+        gg = conv(gc_s, cg_s, lambda k: tb_s[1, k], backward, zero)
+
+        def correlate(grad, get, offsets):
+            def block(b, sums):
+                j0 = b * BLOCK
+                sums = dict(zip(offsets, sums))
+                grads = [grad(j0 + (HALO + j)) for j in range(BLOCK)]
+                for i in range(offsets[0], BLOCK + offsets[-1]):
+                    v = get(j0 + (HALO + i))
+                    for j in range(BLOCK):
+                        if i - j in sums:
+                            sums[i - j] = sums[i - j] + grads[j] * v
+                return tuple(sums[m] for m in offsets)
+
+            sums = lax.fori_loop(0, SPAN // BLOCK, block, (zero,) * len(offsets))
+            return dict(zip(offsets, sums))
+
+        even = correlate(lambda j: gc_s[0, j] - gc_s[1, j - 1], lambda j: xh[0, j], evens)
+        for m in evens:
+            tb_s[0, even_tap(m)] = even[m]
+        odd = correlate(lambda j: gc_s[0, j] - gc_s[1, j], lambda j: xh[1, j], odds)
+        for m in odds:
+            tb_s[0, odd_tap(m)] = odd[m]
+        both = correlate(lambda j: gc_s[1, j], lambda j: cx_s[j], odds)
+        for m in odds:
+            tb_s[0, odd_tap(m)] = tb_s[0, odd_tap(m)] + both[m]
+            if m in evens:
+                tb_s[0, even_tap(m)] = tb_s[0, even_tap(m)] + both[m]
         base = lax.div(ct, 3) * Q_ROWS + lax.rem(ct, 3) * (depth + TAPS + 1) + depth
         gain_row = gain_ref[ct]
-        tail = [jnp.sum(v, axis=0, keepdims=True) * gain_row for v in sums]
+        tail = [jnp.sum(tb_s[0, k], axis=0, keepdims=True) * gain_row for k in range(TAPS)]
         tail.append(jnp.sum(gg, axis=0, keepdims=True))
         out_ref[pl.ds(pl.multiple_of(base, SUB), TAPS + 1), :] = jnp.concatenate(tail, axis=0)
         return loss
@@ -201,7 +249,7 @@
             jax.ShapeDtypeStruct((tiles // 3 * Q_ROWS, LANES), f32),
             jax.ShapeDtypeStruct((1, 1), f32),
         ),
-        in_specs=[vm] * 5,
+        in_specs=[pl.BlockSpec(memory_space=pltpu.HBM)] * 5,
         out_specs=(vm, vm),
         scratch_shapes=[
             pltpu.VMEM((2, ROWS, tiles * LANES), f32),
@@ -214,6 +262,17 @@
             pltpu.VMEM(rows, f32),
             pltpu.VMEM((2 * ROWS, tiles * LANES), bf16),
             pltpu.VMEM((depth, 2 * ROWS), bf16),
+            pltpu.VMEM((2, TAPS, SUB, LANES), f32),
+            pltpu.VMEM((SPAN + 2 * HALO, SUB, LANES), f32),
+            pltpu.VMEM((SPAN + 2 * HALO, SUB, LANES), f32),
+            pltpu.VMEM((SPAN + 1, SUB, LANES), f32),
+            pltpu.VMEM((SPAN, SUB, LANES), f32),
+            pltpu.VMEM(frames.shape, bf16),
+            pltpu.VMEM(above.shape, bf16),
+            pltpu.VMEM(proj.shape, bf16),
+            pltpu.VMEM(gain_tiles.shape, f32),
+            pltpu.VMEM(tap_tiles.shape, f32),
+            pltpu.SemaphoreType.DMA((5,)),
         ],
         compiler_params=pltpu.CompilerParams(vmem_limit_bytes=56 << 20),
         name="module_terms",
@@ -221,10 +280,11 @@
 
 
 def exchange_kernel(
-    cache_ref, want_ref, take_ref, utt_ref, tpos_ref, up_ref, w_ref, taps_ref, gain_ref,
+    cache_hbm, want_hbm, take_hbm, utt_hbm, up_hbm, w_ref, taps_ref, gain_ref,
     fr_ref, above_ref, proj_ref, tapt_ref, gaint_ref,
     pick_s, send_s, arr_s, taps_s, gain_s,
-    row_s, row_r, par_s, par_r,
+    cache_ref, want_ref, take_ref, utt_ref, up_ref,
+    row_s, row_r, par_s, par_r, in_sem,
 ):
     f32, bf16 = jnp.float32, jnp.bfloat16
     peers = arr_s.shape[0]
@@ -236,6 +296,20 @@
     def peer(o):
         return lax.rem(p + o, peers)
 
+    own = pl.ds(pl.multiple_of(f * cols, LANES), cols)
+    loads = [
+        pltpu.make_async_copy(src, dst, in_sem.at[i])
+        for i, (src, dst) in enumerate(
+            [
+                (want_hbm, want_ref), (cache_hbm, cache_ref), (take_hbm, take_ref),
+                (utt_hbm, utt_ref), (up_hbm, up_ref), (w_ref, proj_ref.at[:, own]),
+                (taps_ref, taps_s.at[:, own]), (gain_ref, gain_s.at[:, own]),
+            ]
+        )
+    ]
+    for load in loads:
+        load.start()
+
     barrier = pltpu.get_barrier_semaphore()
 
     def greet(o, carry):
@@ -250,6 +324,8 @@
 
     count, width = cache_ref.shape
     half = width // 2
+    loads[0].wait()
+    loads[1].wait()
     want = jnp.concatenate([want_ref[...], want_ref[...]], axis=0)
     cache_ids = lax.broadcasted_iota(jnp.int32, (SUB, count), 1)
     for d in range(0, peers, 2):
@@ -305,25 +381,27 @@
         for copy in param_copies(o):
             copy.start()
     arr_s[p] = send_s[p]
-    own = pl.ds(pl.multiple_of(f * cols, LANES), cols)
-    proj_ref[:, own] = w_ref[...]
-    taps_s[:, own] = taps_ref[...]
-    gain_s[:, own] = gain_ref[...]
+    for load in loads[2:]:
+        load.wait()
 
     sub = lax.broadcasted_iota(jnp.int32, (SUB, 1), 0)
-    steps = tpos_ref.shape[1]
+    steps = up_ref.shape[0]
     slots = take_ref.shape[1]
     place = lax.broadcasted_iota(jnp.int32, (1, slots), 1) + GAP * utt_ref[...]
-    place = jnp.broadcast_to(place, (SUB, slots))
+    place = jnp.broadcast_to(jnp.where(take_ref[...] >= 0, place, -1), (SUB, slots))
     take = jnp.broadcast_to(take_ref[...], (SUB, slots))
-    tpos = jnp.broadcast_to(tpos_ref[...], (SUB, steps))
+    for j in range(0, SPAN, 2):
+        two = [(place == sub * SPAN + (j + k)).astype(f32) for k in range(2)]
+        pick_s[j * SUB : (j + 2) * SUB, steps : steps + slots] = (
+            jnp.concatenate(two, axis=0).astype(bf16)
+        )
+    slot_ids = lax.broadcasted_iota(jnp.int32, (slots, steps), 0)
+    step_ids = lax.broadcasted_iota(jnp.int32, (slots, steps), 1)
     for h in range(2):
-        for j in range(0, SPAN, 2):
-            two = [
-                (tpos == 2 * (sub * SPAN + (j + k)) + h).astype(f32) for k in range(2)
-            ]
-            row = h * ROWS + j * SUB
-            pick_s[row : row + 2 * SUB, :steps] = jnp.concatenate(two, axis=0).astype(bf16)
+        spread = (step_ids == 2 * slot_ids + h).astype(f32).astype(bf16)
+        pick_s[h * ROWS : (h + 1) * ROWS, :steps] = jnp.dot(
+            pick_s[:ROWS, steps : steps + slots], spread, preferred_element_type=f32
+        ).astype(bf16)
     for r in range(0, 2 * ROWS, ROWS // 2):
         above_ref[r : r + ROWS // 2, :] = jnp.dot(
             pick_s[r : r + ROWS // 2, :steps], up_ref[...], preferred_element_type=f32
@@ -373,11 +451,6 @@
     f32, bf16, i32 = jnp.float32, jnp.bfloat16, jnp.int32
     peers = wanted.shape[0]
     slots = take.shape[0]
-    step = lax.iota(i32, 2 * slots)
-    place = lax.iota(i32, slots) + GAP * utt
-    tpos = jnp.where(
-        jnp.repeat(take, 2) >= 0, 2 * jnp.repeat(place, 2) + step % 2, -1
-    )
     depth, cols = in_proj.shape
     width = cols * members
     tiles = width // LANES
@@ -394,7 +467,7 @@
             shape((tiles, TAPS, LANES), f32),
             shape((tiles, 1, LANES), f32),
         ),
-        in_specs=[vm] * 9,
+        in_specs=[pl.BlockSpec(memory_space=pltpu.HBM)] * 8,
         out_specs=(vm,) * 5,
         scratch_shapes=[
             pltpu.VMEM((max(2 * ROWS, peers * SUB), peers * SUB), bf16),
@@ -402,22 +475,28 @@
             pltpu.VMEM((peers, SUB, half), bf16),
             pltpu.VMEM((TAPS, width), bf16),
             pltpu.VMEM((1, width), bf16),
+            pltpu.VMEM(cache_rows.shape, bf16),
+            pltpu.VMEM(wanted.shape[::-1], i32),
+            pltpu.VMEM((1, slots), i32),
+            pltpu.VMEM((1, slots), i32),
+            pltpu.VMEM(upstream.shape, bf16),
             dma, dma,
             dma((3 * (members - 1),)), dma((3 * (members - 1),)),
+            dma((8,)),
         ],
         compiler_params=pltpu.CompilerParams(
-            collective_id=1, has_side_effects=True, vmem_limit_bytes=40 << 20
+            collective_id=1, has_side_effects=True, vmem_limit_bytes=56 << 20
         ),
         name="exchange",
     )(
-        cache_rows, wanted.T, take[None, :], utt[None, :], tpos[None, :], upstream,
+        cache_rows, wanted.T, take[None, :], utt[None, :], upstream,
         in_proj, taps, gain[None, :],
     )
 
 
 def reduce_kernel(
     g_ref, o_ref,
-    cbuf, ysend, ystage, yfirst, yfrom,
+    gown, own_sem, cbuf, ysend, ystage, yfirst, yfrom,
     xbuf, xstage, xfirst, xfrom,
     zbuf, zfrom, final,
     core_s, core_r, y_s, y_r, x_s, x_r, z_s, z_r, za_s, za_r, xa_s, xa_r, ya_s, ya_r,
@@ -473,12 +552,20 @@
         core_copies.append(
             send(g_ref.at[piece(yy, 1 - core)], cbuf.at[o], core_s.at[o], core_r.at[o], dev_core)
         )
+    own_loads = {}
+    for o in (2, 1, 3, 0):
+        own_loads[o] = pltpu.make_async_copy(
+            g_ref.at[piece(lax.rem(y + o, RING), core)], gown.at[o], own_sem.at[o]
+        )
+        own_loads[o].start()
     half = Y_ROWS // 2
     lo, hi = pl.ds(0, half), pl.ds(half, half)
 
     def summed(o):
-        return g_ref[piece(lax.rem(y + o, RING), core)] + cbuf[o]
-
+        return gown[o] + cbuf[o]
+
+    for load in own_loads.values():
+        load.wait()
     core_copies[0].wait_recv()
     ysend[1] = summed(2).astype(jnp.bfloat16)
     y0 = send(ysend.at[1, lo], yfirst.at[0], y_s.at[0], y_r.at[0], dev_yr)
@@ -491,11 +578,11 @@
     y3 = send(ysend.at[2, lo], yfrom.at[1, lo], y_s.at[3], y_r.at[3], dev_yl)
     core_copies[3].wait_recv()
     y0.wait_recv()
-    part = g_ref[piece(y_r1, core)] + cbuf[1]
+    part = summed(1)
     ystage[0] = (part[:half] + yfirst[0].astype(jnp.float32)).astype(jnp.bfloat16)
     y4 = send(ystage.at[0], yfrom.at[0, lo], y_s.at[4], y_r.at[4], dev_yr)
     y1.wait_recv()
-    part = g_ref[piece(y_l1, core)] + cbuf[3]
+    part = summed(3)
     ystage[1] = (part[half:] + yfirst[1].astype(jnp.float32)).astype(jnp.bfloat16)
     y5 = send(ystage.at[1], yfrom.at[1, hi], y_s.at[5], y_r.at[5], dev_yl)
     for copy in (y2, y3, y4, y5):
@@ -621,9 +708,11 @@
     return pl.pallas_call(
         reduce_kernel,
         out_shape=jax.ShapeDtypeStruct((rows, cols), f32),
-        in_specs=[pl.BlockSpec(memory_space=pltpu.VMEM)],
+        in_specs=[pl.BlockSpec(memory_space=pltpu.HBM)],
         out_specs=pl.BlockSpec(memory_space=pltpu.VMEM),
         scratch_shapes=[
+            pltpu.VMEM((RING, Y_ROWS, LANES), f32),
+            dma((RING,)),
             pltpu.VMEM((RING, Y_ROWS, LANES), f32),
             pltpu.VMEM((3, Y_ROWS, LANES), bf16),
             pltpu.VMEM((2, half, LANES), bf16),
@@ -645,7 +734,7 @@
             dma((4,)), dma((4,)),
         ],
         compiler_params=pltpu.CompilerParams(
-            collective_id=0, has_side_effects=True, vmem_limit_bytes=40 << 20
+            collective_id=0, has_side_effects=True, vmem_limit_bytes=56 << 20
         ),
         name="reduce_gradients",
     )(packed)

time: 187 us -> 170 us (0.909)
  the two profiles are of different devices: /device:TPU:2 before, /device:TPU:8 now
where the time goes in v4:
time: 170 us
  Pallas kernels  163 us (96%)
  local copies, waits for them, and re-layouts  6.04 us (4%)
    pallas_call x1, Pallas kernels, exchange(): pl.pallas_call(exchange_kernel, out_shape=(shape((2 * ROWS, half), bf16),...  69.2 us
    pallas_call x1, Pallas kernels, reduce_gradients(): pl.pallas_call(reduce_kernel, out_shape=jax.ShapeDtypeStruct((rows, cols)...  54.5 us
    pallas_call x1, Pallas kernels, module_terms(): pl.pallas_call(module_kernel, out_shape=(jax.ShapeDtypeStruct((tiles // 3...  39.6 us

profile of v4, /device:TPU:8, one launch (start us, length us, event | category | flops | bytes accessed | tf_op | source)
XLA Modules:
  0.0 170.0 jit_solution(8631092417535155476)
XLA Ops:
  0.6 1.2 broadcast_in_dim.3.gain_ref
  1.9 69.2 %exchange.1 = (bf16[672,512]{1,0:T(8,128)(2,1)}, bf16[672,1536]{1,0:T(8,128)(2,1)}, bf16[512,1536]{1,0:T(8,128)(2,1)}, f32[12,31,128]{2,1,0:T(8,128)}, f32[12,1,128]{2,1,0:T(1,128)}) custom-call(bf16[256,1024]{1,0:T(8,128)(2,1)} %bitcast.8, s32[4,128]{1,0:T(4,128)} %bitcast.9, s32[1,256]{1,0:T(1,128)} %bitcast.10, s32[1,256]{1,0:T(1,128)} %bitcast.11, ...), custom_call_target="tpu_custom_call" | custom-call | tf_op jit(solution)/shard_map/exchange/pallas_call | solution.py:461
  71.1 39.6 %module_terms.1 = (f32[6656,128]{1,0:T(8,128)}, f32[1,1]{1,0:T(1,128)}) custom-call(bf16[672,512]{1,0:T(8,128)(2,1)} %get-tuple-element.11.fr_hbm, bf16[672,1536]{1,0:T(8,128)(2,1)} %get-tuple-element.12.up_hbm, bf16[512,1536]{1,0:T(8,128)(2,1)} %get-tuple-element.13.w_hbm, f32[12,1,128]{2,1,0:T(1,128)} %get-tuple-element.14.gain_hbm, ...), custom_call_target="tpu_custom_call" | custom-call | tf_op jit(solution)/shard_map/module_terms/pallas_call | solution.py:246
  110.7 54.5 %reduce_gradients.1 = f32[544,384]{1,0:T(8,128)} custom-call(f32[6656,128]{1,0:T(8,128)} %get-tuple-element.16.g_ref), custom_call_target="tpu_custom_call" | custom-call | tf_op jit(solution)/shard_map/reduce_gradients/pallas_call | solution.py:708
  165.2 1.3 slice_reduce_fusion
  166.5 1.4 slice.10
  167.9 2.1 %slice.9 = f32[512,384]{1,0:T(8,128)} slice(f32[544,384]{1,0:T(8,128)} %reduce_gradients.1), slice={[0:512], [0:384]} | slice | bytes 1572864 | tf_op jit(solution)/shard_map/slice | solution.py:754

commit v5 on v4

--- a/solution.py
+++ b/solution.py
@@ -281,10 +281,10 @@
 
 def exchange_kernel(
     cache_hbm, want_hbm, take_hbm, utt_hbm, up_hbm, w_ref, taps_ref, gain_ref,
-    fr_ref, above_ref, proj_ref, tapt_ref, gaint_ref,
-    pick_s, send_s, arr_s, taps_s, gain_s,
+    fr_ref, above_hbm, proj_hbm, tapt_ref, gaint_ref,
+    above_ref, proj_ref, pick_s, send_s, arr_s, taps_s, gain_s,
     cache_ref, want_ref, take_ref, utt_ref, up_ref,
-    row_s, row_r, par_s, par_r, in_sem,
+    row_s, row_r, par_s, par_r, in_sem, out_sem,
 ):
     f32, bf16 = jnp.float32, jnp.bfloat16
     peers = arr_s.shape[0]
@@ -422,6 +422,12 @@
     for o in range(1, members):
         for copy in param_copies(o):
             copy.wait_recv()
+    leaving = [
+        pltpu.make_async_copy(above_ref, above_hbm, out_sem.at[0]),
+        pltpu.make_async_copy(proj_ref, proj_hbm, out_sem.at[1]),
+    ]
+    for copy in leaving:
+        copy.start()
     tiles = gaint_ref.shape[0]
     for c in range(tiles):
         lanes = slice(c * LANES, (c + 1) * LANES)
@@ -445,6 +451,8 @@
     for o in range(1, members):
         for copy in param_copies(o):
             copy.wait_send()
+    for copy in leaving:
+        copy.wait()
 
 
 def exchange(cache_rows, wanted, take, utt, upstream, in_proj, taps, gain, members):
@@ -468,8 +476,16 @@
             shape((tiles, 1, LANES), f32),
         ),
         in_specs=[pl.BlockSpec(memory_space=pltpu.HBM)] * 8,
-        out_specs=(vm,) * 5,
+        out_specs=(
+            vm,
+            pl.BlockSpec(memory_space=pltpu.HBM),
+            pl.BlockSpec(memory_space=pltpu.HBM),
+            vm,
+            vm,
+        ),
         scratch_shapes=[
+            pltpu.VMEM((2 * ROWS, width), bf16),
+            pltpu.VMEM((depth, width), bf16),
             pltpu.VMEM((max(2 * ROWS, peers * SUB), peers * SUB), bf16),
             pltpu.VMEM((peers, SUB, half), bf16),
             pltpu.VMEM((peers, SUB, half), bf16),
@@ -483,6 +499,7 @@
             dma, dma,
             dma((3 * (members - 1),)), dma((3 * (members - 1),)),
             dma((8,)),
+            dma((2,)),
         ],
         compiler_params=pltpu.CompilerParams(
             collective_id=1, has_side_effects=True, vmem_limit_bytes=56 << 20
@@ -495,7 +512,7 @@
 
 
 def reduce_kernel(
-    g_ref, o_ref,
+    g_ref, proj_ref, taps_ref, gain_ref,
     gown, own_sem, cbuf, ysend, ystage, yfirst, yfrom,
     xbuf, xstage, xfirst, xfrom,
     zbuf, zfrom, final,
@@ -680,11 +697,15 @@
     for copy in (b0, b1, b2, b3):
         copy.wait_recv()
 
-    tile_rows = o_ref.shape[0]
-    for i in range(o_ref.shape[1] // LANES):
-        o_ref[:, i * LANES : (i + 1) * LANES] = final[
-            i * tile_rows : (i + 1) * tile_rows
-        ].astype(jnp.float32)
+    depth, cols = proj_ref.shape
+    tile_rows = depth + TAPS + 1
+    for i in range(cols // LANES):
+        lanes = slice(i * LANES, (i + 1) * LANES)
+        top = i * tile_rows
+        proj_ref[:, lanes] = final[top : top + depth].astype(jnp.float32)
+        tail = final[top + depth : top + tile_rows].astype(jnp.float32)
+        taps_ref[:, lanes] = tail[:TAPS]
+        gain_ref[:, lanes] = tail[TAPS:]
 
     for copy in core_copies + [y0, y1, y2, y3, y4, y5, x0, x1, x2, x3, x4, x5]:
         copy.wait_send()
@@ -707,9 +728,11 @@
     dma = pltpu.SemaphoreType.DMA
     return pl.pallas_call(
         reduce_kernel,
-        out_shape=jax.ShapeDtypeStruct((rows, cols), f32),
+        out_shape=tuple(
+            jax.ShapeDtypeStruct((size, cols), f32) for size in (rows - TAPS - 1, TAPS, 1)
+        ),
         in_specs=[pl.BlockSpec(memory_space=pltpu.HBM)],
-        out_specs=pl.BlockSpec(memory_space=pltpu.VMEM),
+        out_specs=(pl.BlockSpec(memory_space=pltpu.VMEM),) * 3,
         scratch_shapes=[
             pltpu.VMEM((RING, Y_ROWS, LANES), f32),
             dma((RING,)),
@@ -734,7 +757,7 @@
             dma((4,)), dma((4,)),
         ],
         compiler_params=pltpu.CompilerParams(
-            collective_id=0, has_side_effects=True, vmem_limit_bytes=56 << 20
+            collective_id=0, has_side_effects=True, vmem_limit_bytes=61 << 20
         ),
         name="reduce_gradients",
     )(packed)
@@ -749,13 +772,8 @@
     )
     packed, device_loss = module_terms(*moved)
     depth, cols = in_proj.shape
-    total = reduce_gradients(packed, depth + TAPS + 1, cols)
-    return (
-        total[:depth],
-        total[depth : depth + TAPS],
-        total[depth + TAPS],
-        device_loss,
-    )
+    grad_proj, grad_taps, grad_gain = reduce_gradients(packed, depth + TAPS + 1, cols)
+    return (grad_proj, grad_taps, grad_gain[0], device_loss)
 
 
 def solution(mesh):

time: 170 us -> 169 us (level)
    slice x3 -> x0, local copies, waits for them, and re-layouts: 4.8 us -> none  [the longest x1 2.06 us: per_device(): total[:depth]]
    unnamed x0 -> x2, local copies, waits for them, and re-layouts: none -> 3.48 us
where the time goes in v5:
time: 169 us
  Pallas kernels  162 us (96%)
  local copies, waits for them, and re-layouts  4.73 us (3%)
    pallas_call x1, Pallas kernels, exchange(): pl.pallas_call(exchange_kernel, out_shape=(shape((2 * ROWS, half), bf16),...  68 us
    pallas_call x1, Pallas kernels, reduce_gradients(): pl.pallas_call(reduce_kernel, out_shape=tuple((jax.ShapeDtypeStruct((size...  54.5 us
    pallas_call x1, Pallas kernels, module_terms(): pl.pallas_call(module_kernel, out_shape=(jax.ShapeDtypeStruct((tiles // 3...  39.6 us
    unnamed x2, local copies, waits for them, and re-layouts  3.48 us

profile of v5, /device:TPU:8, one launch (start us, length us, event | category | flops | bytes accessed | tf_op | source)
XLA Modules:
  0.0 168.8 jit_solution(7487789998119805094)
XLA Ops:
  0.6 1.2 broadcast_in_dim.3.gain_ref
  1.9 68.0 %exchange.1 = (bf16[672,512]{1,0:T(8,128)(2,1)}, bf16[672,1536]{1,0:T(8,128)(2,1)}, bf16[512,1536]{1,0:T(8,128)(2,1)}, f32[12,31,128]{2,1,0:T(8,128)}, f32[12,1,128]{2,1,0:T(1,128)}) custom-call(bf16[256,1024]{1,0:T(8,128)(2,1)} %bitcast.8, s32[4,128]{1,0:T(4,128)} %bitcast.9, s32[1,256]{1,0:T(1,128)} %bitcast.10, s32[1,256]{1,0:T(1,128)} %bitcast.11, ...), custom_call_target="tpu_custom_call" | custom-call | tf_op jit(solution)/shard_map/exchange/pallas_call | solution.py:469
  69.9 39.6 %module_terms.1 = (f32[6656,128]{1,0:T(8,128)}, f32[1,1]{1,0:T(1,128)}) custom-call(bf16[672,512]{1,0:T(8,128)(2,1)} %get-tuple-element.14.fr_hbm, bf16[672,1536]{1,0:T(8,128)(2,1)} %get-tuple-element.15.up_hbm, bf16[512,1536]{1,0:T(8,128)(2,1)} %get-tuple-element.16.w_hbm, f32[12,1,128]{2,1,0:T(1,128)} %get-tuple-element.17.gain_hbm, ...), custom_call_target="tpu_custom_call" | custom-call | tf_op jit(solution)/shard_map/module_terms/pallas_call | solution.py:246
  109.5 54.5 %reduce_gradients.1 = (f32[512,384]{1,0:T(8,128)}, f32[31,384]{1,0:T(8,128)}, f32[1,384]{1,0:T(1,128)}) custom-call(f32[6656,128]{1,0:T(8,128)} %get-tuple-element.19.g_ref), custom_call_target="tpu_custom_call" | custom-call | tf_op jit(solution)/shard_map/reduce_gradients/pallas_call | solution.py:729
  164.0 1.3 reduce
  165.3 2.1 %copy.14 = f32[512,384]{1,0:T(8,128)} copy(f32[512,384]{1,0:T(8,128)} %get-tuple-element.28) | data formatting | bytes 1572864
  167.4 1.4 copy.15
